TPU v7x, 256 devices: a whole 4x4x8 slice. The times are simulated.
256 devices in a mesh: plate: 8 (over y, x_lo), sub: 32 (over x_hi, z, core).
Axes of the slice: x: 4 (x_hi: 2, x_lo: 2; x = x_hi * 2 + x_lo), y: 4, z: 8, core: 2. Of those that a mesh axis runs over, the one named last changes fastest.
Arguments:
- populations: float32 [19, 32, 512, 128], P(None, 'plate', 'sub'), may hold values from 0.5 to 1.5
- solid: int32 [32, 512, 128], P('plate', 'sub'), may hold values 0 or 1
- marker_corner: int32 [3, 16384], P(None, ('plate', 'sub')), may hold values from 0 to 508, as said below
- marker_frac: float32 [3, 16384], P(None, ('plate', 'sub')), may hold values from 0 to 1
- marker_target: float32 [3, 16384], P(None, ('plate', 'sub')), may hold values from -0.6 to 0.6
- stiffness: float32 [16384], P(('plate', 'sub')), may hold values from 0.5 to 4
- displacement: float32 [3, 16384], P(None, ('plate', 'sub')), may hold values from -0.6 to 0.6
Outputs:
- populations_out: float32 [19, 32, 512, 128], P(None, 'plate', 'sub')
- displacement_out: float32 [3, 16384], P(None, ('plate', 'sub'))
- marker_force: float32 [3, 16384], P(None, ('plate', 'sub'))
Inputs may be any that keep to these rules, and one draw needn't show every extreme that they name: `marker_corner`: components are the first cell of the stencil along the three dimensions. Every stencil lies inside the grid without wrapping, and along the first dimension inside the slab of 4 cells that its plate's markers share; the markers of plate p are rows p * 2048 to (p + 1) * 2048 - 1 and lie in slab p.
All inputs are finite; a program needn't handle non-finite values. No bound on the sum of `solid` on one device may be relied on, other than what follows from the above.
Results may differ from a plain program's by a relative error of at most 0.00011.
Values sent between devices are 32-bit elements; how exact they have to be, the bound alone decides.
No kernel may reach another device: no remote copies, remote signals or barrier semaphores. Data moves between devices by JAX's collectives and lax.ppermute only.
A program may use at most 64 MiB of HBM per device.

v0:
```python
import jax
import jax.numpy as jnp
from jax import lax
from jax.sharding import PartitionSpec as P

STEPS = 2


DIRS = [
    (0, 0, 0),
    (1, 0, 0),
    (-1, 0, 0),
    (0, 1, 0),
    (0, -1, 0),
    (0, 0, 1),
    (0, 0, -1),
    (1, 1, 0),
    (-1, -1, 0),
    (1, -1, 0),
    (-1, 1, 0),
    (1, 0, 1),
    (-1, 0, -1),
    (1, 0, -1),
    (-1, 0, 1),
    (0, 1, 1),
    (0, -1, -1),
    (0, 1, -1),
    (0, -1, 1),
]
WEIGHTS = [1.0 / 3.0] + [1.0 / 18.0] * 6 + [1.0 / 36.0] * 12
OPPOSITE = [0, 2, 1, 4, 3, 6, 5, 8, 7, 10, 9, 12, 11, 14, 13, 16, 15, 18, 17]
KAPPA = 4.0
RELAX = 0.9


def extended(x, sides, width):
    for axis, dim in sides:
        peers, length = (lax.axis_size(axis), x.shape[dim])
        up = [(i, (i + 1) % peers) for i in range(peers)]
        down = [(j, i) for i, j in up]
        last = lax.slice_in_dim(x, length - width, length, axis=dim)
        initial = lax.slice_in_dim(x, 0, width, axis=dim)
        before = lax.ppermute(last, axis, up)
        after = lax.ppermute(initial, axis, down)
        x = jnp.concatenate([before, x, after], axis=dim)
    return x


def kernel_weights(frac):
    root = jnp.sqrt(1.0 + 4.0 * frac - 4.0 * frac * frac)
    second = (3.0 - 2.0 * frac + root) / 8.0
    third = (1.0 + 2.0 * frac + root) / 8.0
    return jnp.stack([0.5 - third, second, third, 0.5 - second])


def dense_rows(first, weights, length):
    cells = jnp.arange(length, dtype=jnp.int32)[:, None]
    result = jnp.zeros((length, first.shape[0]), jnp.float32)
    for offset in range(4):
        result = result + weights[offset][None, :] * (cells == (first + offset)[None, :]).astype(
            jnp.float32
        )
    return result


def moments(pops):
    density = jnp.sum(pops, 0)
    comps = []
    for axis in range(3):
        total = jnp.zeros_like(density)
        for index in range(19):
            if DIRS[index][axis] == 1:
                total = total + pops[index]
            elif DIRS[index][axis] == -1:
                total = total - pops[index]
        comps.append(total)
    return (density, jnp.stack(comps) / density)


def dotted(index, vectors):
    total = jnp.zeros_like(vectors[0])
    for axis in range(3):
        if DIRS[index][axis] == 1:
            total = total + vectors[axis]
        elif DIRS[index][axis] == -1:
            total = total - vectors[axis]
    return total


def collide(pops, density, velocity, spread, fluid):
    speed_sq = jnp.sum(velocity * velocity, 0)
    result = []
    for index in range(19):
        proj = dotted(index, velocity)
        equil = WEIGHTS[index] * density * (1.0 + 3.0 * proj + 4.5 * proj * proj - 1.5 * speed_sq)
        post = (
            pops[index]
            - (pops[index] - equil) / RELAX
            + 3.0 * WEIGHTS[index] * dotted(index, spread)
        )
        result.append(jnp.where(fluid, post, pops[OPPOSITE[index]]))
    return jnp.stack(result)


def padded_post(post):
    return extended(post, (("plate", 1), ("sub", 2)), 1)


def stream_cells(padded, size_x, size_y):
    result = []
    for index in range(19):
        shift_x, shift_y, shift_z = DIRS[index]
        moved = padded[
            index, 1 - shift_x : 1 - shift_x + size_x, 1 - shift_y : 1 - shift_y + size_y, :
        ]
        result.append(jnp.roll(moved, shift_z, axis=2))
    return jnp.stack(result)


def shards(populations, solid, marker_corner, marker_frac, marker_target, stiffness, displacement):
    count, size_x, size_y, size_z = populations.shape
    corners = lax.all_gather(marker_corner, "sub", axis=1, tiled=True)
    fracs = lax.all_gather(marker_frac, "sub", axis=1, tiled=True)
    x_first = corners[0] - lax.axis_index("plate") * size_x
    y_first = corners[1] - lax.axis_index("sub") * size_y
    x_rows = dense_rows(x_first, kernel_weights(fracs[0]), size_x)
    y_rows = dense_rows(y_first, kernel_weights(fracs[1]), size_y)
    z_rows = dense_rows(corners[2], kernel_weights(fracs[2]), size_z)
    plate_count = x_rows.shape[1]
    xy_rows = (x_rows[:, None, :] * y_rows[None, :, :]).reshape(size_x * size_y, plate_count)
    fluid = solid == 0
    target_now, spring_now, disp = (marker_target, stiffness, displacement)
    force = jnp.zeros_like(disp)
    pops = populations
    for step in range(STEPS):
        density, velocity = moments(pops)
        flat = velocity.reshape(3, size_x * size_y, size_z)
        along_z = jnp.einsum("kcz,zm->kcm", flat, z_rows, precision=lax.Precision.HIGHEST)
        partial_value = jnp.sum(along_z * xy_rows[None], 1)
        marker_vel = lax.psum_scatter(partial_value, "sub", scatter_dimension=1, tiled=True)
        force = KAPPA * (target_now - marker_vel) - spring_now[None] * disp
        disp = disp + marker_vel
        plate_force = lax.all_gather(force, "sub", axis=1, tiled=True)
        weighted = xy_rows[None] * plate_force[:, None, :]
        spread = jnp.einsum("kcm,zm->kcz", weighted, z_rows, precision=lax.Precision.HIGHEST)
        spread = spread.reshape(3, size_x, size_y, size_z)
        post = collide(pops, density, velocity, spread, fluid)
        pops = stream_cells(padded_post(post), size_x, size_y)
    return (pops, disp, force)


def solution(mesh):
    in_specs = (
        P(None, "plate", "sub", None),
        P("plate", "sub", None),
        P(None, ("plate", "sub")),
        P(None, ("plate", "sub")),
        P(None, ("plate", "sub")),
        P(("plate", "sub")),
        P(None, ("plate", "sub")),
    )
    out_specs = (
        P(None, "plate", "sub", None),
        P(None, ("plate", "sub")),
        P(None, ("plate", "sub")),
    )
    return jax.shard_map(shards, mesh=mesh, in_specs=in_specs, out_specs=out_specs, check_vma=False)
```

profile of v0, /device:TPU:8, one launch (start us, length us, event | category | flops | bytes accessed | tf_op | source)
XLA Modules:
  0.0 458.1 jit_solution(3523056900203541234)
XLA Ops:
  7.2 1.0 add_subtract_fusion.3
  8.2 0.9 add_subtract_fusion.2
  9.2 0.9 subtract_add_fusion
  10.1 44.9 %all-gather.1 = f32[32,64,3]{1,2,0:T(4,128)S(1)} all-gather(f32[1,64,3]{1,2,0:T(4,128)S(1)} %bitcast.850), channel_id=1, replica_groups=mesh['plate'=8,'sub'=32] {'sub'}, dimensions={0}, use_global_device_ids=true | all-gather | bytes 25344 | tf_op jit(solution)/shard_map/all_gather | solution.py:123
  55.2 36.9 %all-gather = s32[32,64,3]{1,2,0:T(4,128)S(1)} all-gather(s32[1,64,3]{1,2,0:T(4,128)S(1)} %bitcast.851), channel_id=1, replica_groups=mesh['plate'=8,'sub'=32] {'sub'}, dimensions={0}, use_global_device_ids=true | all-gather | bytes 25344 | tf_op jit(solution)/shard_map/all_gather | solution.py:122
  92.5 1.9 fusion.4
  94.5 1.4 copy.78
  96.0 111.6 %reduce-scatter.7.cloned.1.call-done = f32[64,3]{1,0:T(8,128)} async-done(((f32[2048,3]{1,0:T(8,128)}), f32[64,3]{1,0:T(8,128)}) %reduce-scatter.7.cloned.1.call-update) | async-done | bytes 784
  207.7 0.8 copy.79
  208.5 39.1 %all-gather.2 = f32[32,64,3]{1,2,0:T(4,128)S(1)} all-gather(f32[1,64,3]{1,2,0:T(4,128)S(1)} %subtract_bitcast_fusion), channel_id=1, replica_groups=mesh['plate'=8,'sub'=32] {'sub'}, dimensions={0}, use_global_device_ids=true | all-gather | bytes 25344 | tf_op jit(solution)/shard_map/all_gather | solution.py:143
  247.7 1.9 fusion.2
  250.4 0.8 collective-permute-start
  251.2 2.2 collective-permute-start.1
  253.5 4.8 %collective-permute-done = f32[19,1,16,128]{3,2,1,0:T(8,128)S(1)} collective-permute-done((f32[19,1,16,128]{3,2,1,0:T(8,128)S(1)}, f32[19,1,16,128]{3,2,1,0:T(8,128)S(1)}, u32[]{:S(2)}, u32[]{:S(2)}) %collective-permute-start) | collective-permute-done | bytes 155680 | tf_op jit(solution)/shard_map/ppermute | solution.py:43
  258.3 2.7 collective-permute-done.1
  261.5 5.3 %collective-permute-start.3 = (f32[19,6,1,128]{3,2,1,0:T(1,128)S(1)}, f32[19,6,1,128]{3,2,1,0:T(1,128)S(1)}, u32[]{:S(2)}, u32[]{:S(2)}) collective-permute-start(f32[19,6,1,128]{3,2,1,0:T(1,128)S(1)} %get-tuple-element.72), channel_id=1, source_target_pairs={{1,0},{2,1},{3,2},{4,3},{5,4},{6,5},{7,6},{8,7},{9,8},{10,9},{11,1... | collective-permute-start | bytes 175112 | tf_op jit(solution)/shard_map/ppermute | solution.py:44
  266.9 1.9 collective-permute-done.2
  269.2 0.2 bitcast_add_fusion
  269.8 1.9 fusion.5
  271.7 1.4 copy.80
  273.5 114.1 %reduce-scatter.9.cloned.1.call-done = f32[64,3]{1,0:T(8,128)} async-done(((f32[2048,3]{1,0:T(8,128)}), f32[64,3]{1,0:T(8,128)}) %reduce-scatter.9.cloned.1.call-update) | async-done | bytes 784
  387.5 0.8 copy.81
  388.4 0.6 add_add_fusion
  389.0 39.2 %all-gather.3 = f32[32,64,3]{1,2,0:T(4,128)S(1)} all-gather(f32[1,64,3]{1,2,0:T(4,128)S(1)} %bitcast.849), channel_id=1, replica_groups=mesh['plate'=8,'sub'=32] {'sub'}, dimensions={0}, use_global_device_ids=true | all-gather | bytes 25344 | tf_op jit(solution)/shard_map/all_gather | solution.py:143
  428.2 1.9 fusion
  430.9 0.8 collective-permute-start.4
  431.6 2.2 collective-permute-start.5
  434.0 4.7 %collective-permute-done.4 = f32[19,1,16,128]{3,2,1,0:T(8,128)S(1)} collective-permute-done((f32[19,1,16,128]{3,2,1,0:T(8,128)S(1)}, f32[19,1,16,128]{3,2,1,0:T(8,128)S(1)}, u32[]{:S(2)}, u32[]{:S(2)}) %collective-permute-start.4) | collective-permute-done | bytes 155680 | tf_op jit(solution)/shard_map/ppermute | solution.py:43
  438.7 2.7 collective-permute-done.5
  441.7 5.3 %collective-permute-start.7 = (f32[19,6,1,128]{3,2,1,0:T(1,128)S(1)}, f32[19,6,1,128]{3,2,1,0:T(1,128)S(1)}, u32[]{:S(2)}, u32[]{:S(2)}) collective-permute-start(f32[19,6,1,128]{3,2,1,0:T(1,128)S(1)} %get-tuple-element.68), channel_id=1, source_target_pairs={{1,0},{2,1},{3,2},{4,3},{5,4},{6,5},{7,6},{8,7},{9,8},{10,9},{11,1... | collective-permute-start | bytes 175112 | tf_op jit(solution)/shard_map/ppermute | solution.py:44
  447.0 1.9 collective-permute-done.6
  450.4 0.8 copy-done.1
  (144 shorter events, 5.7 us)
Async XLA Ops:
  7.2 85.0 %copy-start = (f32[19,4,16,128]{3,2,1,0:T(8,128)S(1)}, f32[19,4,16,128]{3,2,1,0:T(8,128)}, u32[]{:S(2)}) copy-start(f32[19,4,16,128]{3,2,1,0:T(8,128)} %param.7) | copy-start | bytes 1867780
  7.2 2.9 copy-start.6
  7.2 48.0 %copy-start.7 = (s32[3,64]{1,0:T(4,128)S(1)}, s32[3,64]{1,0:T(4,128)}, u32[]{:S(2)}) copy-start(s32[3,64]{1,0:T(4,128)} %param.9) | copy-start | bytes 2308
  7.2 200.5 %reduce-scatter.7.cloned.1.call-start = ((), (), s32[]{:S(2)}) async-start(), calls=%async_computation.2 | async-start | bytes 1081344
  94.5 1.5 copy-start.2
  95.9 112.6 %copy-start.3 = (f32[3,64]{1,0:T(4,128)S(1)}, f32[3,64]{1,0:T(4,128)}, u32[]{:S(2)}) copy-start(f32[3,64]{1,0:T(4,128)} %param.13) | copy-start | bytes 2308
  95.9 112.6 %copy-start.4 = (f32[3,64]{1,0:T(4,128)S(1)}, f32[3,64]{1,0:T(4,128)}, u32[]{:S(2)}) copy-start(f32[3,64]{1,0:T(4,128)} %param.11) | copy-start | bytes 2308
  95.9 112.6 %copy-start.8 = (f32[64]{0:T(128)S(1)}, f32[64]{0:T(128)}, u32[]{:S(2)}) copy-start(f32[64]{0:T(128)} %param.12) | copy-start | bytes 772
  95.9 291.6 %reduce-scatter.9.cloned.1.call-start = ((), (), s32[]{:S(2)}) async-start(), calls=%async_computation.3 | async-start | bytes 1081344
  250.4 7.9 %collective-permute-start = (f32[19,1,16,128]{3,2,1,0:T(8,128)S(1)}, f32[19,1,16,128]{3,2,1,0:T(8,128)S(1)}, u32[]{:S(2)}, u32[]{:S(2)}) collective-permute-start(f32[19,1,16,128]{3,2,1,0:T(8,128)S(1)} %get-tuple-element.85), channel_id=1, source_target_pairs={{0,32},{32,64},{64,96},{96,128},{128,160},{160,192},{192,224},{224... | collective-permute-start | bytes 466952 | tf_op jit(solution)/shard_map/ppermute | solution.py:43
  251.2 9.9 %collective-permute-start.1 = (f32[19,1,16,128]{3,2,1,0:T(8,128)S(1)}, f32[19,1,16,128]{3,2,1,0:T(8,128)S(1)}, u32[]{:S(2)}, u32[]{:S(2)}) collective-permute-start(f32[19,1,16,128]{3,2,1,0:T(8,128)S(1)} %get-tuple-element.84), channel_id=1, source_target_pairs={{32,0},{64,32},{96,64},{128,96},{160,128},{192,160},{224,192},{0,2... | collective-permute-start | bytes 466952 | tf_op jit(solution)/shard_map/ppermute | solution.py:44
  261.4 7.3 %collective-permute-start.2 = (f32[19,6,1,128]{3,2,1,0:T(1,128)S(1)}, f32[19,6,1,128]{3,2,1,0:T(1,128)S(1)}, u32[]{:S(2)}, u32[]{:S(2)}) collective-permute-start(f32[19,6,1,128]{3,2,1,0:T(1,128)S(1)} %get-tuple-element.73), channel_id=1, source_target_pairs={{0,1},{1,2},{2,3},{3,4},{4,5},{5,6},{6,7},{7,8},{8,9},{9,10},{10,1... | collective-permute-start | bytes 175112 | tf_op jit(solution)/shard_map/ppermute | solution.py:43
  261.5 7.2 %collective-permute-start.3 = (f32[19,6,1,128]{3,2,1,0:T(1,128)S(1)}, f32[19,6,1,128]{3,2,1,0:T(1,128)S(1)}, u32[]{:S(2)}, u32[]{:S(2)}) collective-permute-start(f32[19,6,1,128]{3,2,1,0:T(1,128)S(1)} %get-tuple-element.72), channel_id=1, source_target_pairs={{1,0},{2,1},{3,2},{4,3},{5,4},{6,5},{7,6},{8,7},{9,8},{10,9},{11,1... | collective-permute-start | bytes 175112 | tf_op jit(solution)/shard_map/ppermute | solution.py:44
  389.0 41.2 %copy-start.5 = (f32[3,64]{1,0:T(4,128)}, f32[3,64]{1,0:T(4,128)S(1)}, u32[]{:S(2)}) copy-start(f32[3,64]{1,0:T(4,128)S(1)} %get-tuple-element.155) | copy-start | bytes 2308
  430.9 7.9 %collective-permute-start.4 = (f32[19,1,16,128]{3,2,1,0:T(8,128)S(1)}, f32[19,1,16,128]{3,2,1,0:T(8,128)S(1)}, u32[]{:S(2)}, u32[]{:S(2)}) collective-permute-start(f32[19,1,16,128]{3,2,1,0:T(8,128)S(1)} %get-tuple-element.82), channel_id=1, source_target_pairs={{0,32},{32,64},{64,96},{96,128},{128,160},{160,192},{192,224},{224... | collective-permute-start | bytes 466952 | tf_op jit(solution)/shard_map/ppermute | solution.py:43
  431.6 9.8 %collective-permute-start.5 = (f32[19,1,16,128]{3,2,1,0:T(8,128)S(1)}, f32[19,1,16,128]{3,2,1,0:T(8,128)S(1)}, u32[]{:S(2)}, u32[]{:S(2)}) collective-permute-start(f32[19,1,16,128]{3,2,1,0:T(8,128)S(1)} %get-tuple-element.81), channel_id=1, source_target_pairs={{32,0},{64,32},{96,64},{128,96},{160,128},{192,160},{224,192},{0,2... | collective-permute-start | bytes 466952 | tf_op jit(solution)/shard_map/ppermute | solution.py:44
  441.6 7.3 %collective-permute-start.6 = (f32[19,6,1,128]{3,2,1,0:T(1,128)S(1)}, f32[19,6,1,128]{3,2,1,0:T(1,128)S(1)}, u32[]{:S(2)}, u32[]{:S(2)}) collective-permute-start(f32[19,6,1,128]{3,2,1,0:T(1,128)S(1)} %get-tuple-element.69), channel_id=1, source_target_pairs={{0,1},{1,2},{2,3},{3,4},{4,5},{5,6},{6,7},{7,8},{8,9},{9,10},{10,1... | collective-permute-start | bytes 175112 | tf_op jit(solution)/shard_map/ppermute | solution.py:43
  441.7 7.2 %collective-permute-start.7 = (f32[19,6,1,128]{3,2,1,0:T(1,128)S(1)}, f32[19,6,1,128]{3,2,1,0:T(1,128)S(1)}, u32[]{:S(2)}, u32[]{:S(2)}) collective-permute-start(f32[19,6,1,128]{3,2,1,0:T(1,128)S(1)} %get-tuple-element.68), channel_id=1, source_target_pairs={{1,0},{2,1},{3,2},{4,3},{5,4},{6,5},{7,6},{8,7},{9,8},{10,9},{11,1... | collective-permute-start | bytes 175112 | tf_op jit(solution)/shard_map/ppermute | solution.py:44
  450.4 0.8 copy-start.1
Sparse Core Ops, SparseCore 0:
  96.0 111.5 reduce-scatter.6
  273.2 114.2 reduce-scatter.8
where the time goes:
time: 459 us; the launch traced here: 458 us
  waiting for transfers between devices  244 us (53%)
  blocking collectives  160 us (35%)
  starting transfers between devices  16.9 us (4%)
  between operations  14.7 us (3%)
  matrix products  7.68 us (2%)
  local copies, waits for them, and re-layouts  7.34 us (2%)
  other arithmetic  6.96 us (2%)
    unnamed x4, waiting for transfers between devices  226 us
    all_gather x2, blocking collectives, shards(): plate_force = lax.all_gather(force, 'sub', axis=1, tiled=True)  78.3 us
    all_gather x1, blocking collectives, shards(): fracs = lax.all_gather(marker_frac, 'sub', axis=1, tiled=True)  44.9 us
    all_gather x1, blocking collectives, shards(): corners = lax.all_gather(marker_corner, 'sub', axis=1, tiled=True)  36.9 us
    ppermute x4, starting transfers between devices, extended(): after = lax.ppermute(initial, axis, down)  15.2 us
    ppermute x4, waiting for transfers between devices, extended(): before = lax.ppermute(last, axis, up)  13.2 us
  transfers between devices with their start and end apart: 10, of which 8 were waited for; matrix products, arithmetic and copies ran while one was open for 0% of the time, Pallas kernels for 0%

commit v1 on v0

v1 whole, which is shorter than its diff:
```python
import functools
import jax
import jax.numpy as jnp
from jax import lax
from jax.experimental import pallas as pl
from jax.experimental.pallas import tpu as pltpu
from jax.sharding import PartitionSpec as P

DIRS = [
    (0, 0, 0),
    (1, 0, 0),
    (-1, 0, 0),
    (0, 1, 0),
    (0, -1, 0),
    (0, 0, 1),
    (0, 0, -1),
    (1, 1, 0),
    (-1, -1, 0),
    (1, -1, 0),
    (-1, 1, 0),
    (1, 0, 1),
    (-1, 0, -1),
    (1, 0, -1),
    (-1, 0, 1),
    (0, 1, 1),
    (0, -1, -1),
    (0, 1, -1),
    (0, -1, 1),
]
WEIGHTS = [1.0 / 3.0] + [1.0 / 18.0] * 6 + [1.0 / 36.0] * 12
KAPPA = 4.0
RELAX = 0.9
UP = [i for i in range(19) if DIRS[i][0] == 1]
DOWN = [i for i in range(19) if DIRS[i][0] == -1]

CX = 4
ROWS = 16
HALO = 8
EXT = ROWS + 2 * HALO
NZ = 128
XY = CX * EXT
TRIM = 4
INNER = EXT - 2 * TRIM
MARKERS = 2048
INSIDE, OUTSIDE = (1, 2), (0, 3)
LANES = 128
F32 = jnp.float32
BF16 = jnp.bfloat16


def split(value):
    high = value.astype(BF16)
    low = (value - high.astype(F32)).astype(BF16)
    return high, low


def moments_of(values):
    density = functools.reduce(lambda a, b: a + b, values)
    inverse = 1.0 / density
    velocity = []
    for axis in range(3):
        plus = functools.reduce(lambda a, b: a + b, [values[i] for i in range(19) if DIRS[i][axis] == 1])
        minus = functools.reduce(lambda a, b: a + b, [values[i] for i in range(19) if DIRS[i][axis] == -1])
        velocity.append((plus - minus) * inverse)
    return density, velocity


def along(index, vectors):
    total = None
    for axis in range(3):
        sign = DIRS[index][axis]
        if sign == 0:
            continue
        if total is None:
            total = vectors[axis] if sign == 1 else -vectors[axis]
        else:
            total = total + vectors[axis] if sign == 1 else total - vectors[axis]
    return total


def relaxed(values, density, velocity, fluid, put):
    keep, rate = 1.0 - 1.0 / RELAX, 1.0 / RELAX
    scaled = density * rate
    base = scaled - 1.5 * scaled * (
        velocity[0] * velocity[0] + velocity[1] * velocity[1] + velocity[2] * velocity[2]
    )
    put(0, jnp.where(fluid, keep * values[0] + WEIGHTS[0] * base, values[0]))
    for index in range(1, 19, 2):
        weight = WEIGHTS[index]
        first, second = values[index], values[index + 1]
        proj = along(index, velocity)
        scaled_proj = scaled * proj
        even = weight * (base + 4.5 * scaled_proj * proj)
        odd = (3.0 * weight) * scaled_proj
        put(index, jnp.where(fluid, keep * first + (even + odd), second))
        put(index + 1, jnp.where(fluid, keep * second + (even - odd), first))


def forced(base, force, put):
    put(0, base(0))
    for index in range(1, 19, 2):
        push = (3.0 * WEIGHTS[index]) * along(index, force)
        put(index, base(index) + push)
        put(index + 1, base(index + 1) - push)


def interpolated(velocity, zcat, planes, cols, rows):
    z_high, z_low = zcat[0:NZ, cols], zcat[NZ : 2 * NZ, cols]
    found = jnp.dot(velocity, jnp.concatenate([z_high, z_high], 0), preferred_element_type=F32)
    found = found + jnp.dot(velocity[:, 0:NZ], z_low, preferred_element_type=F32)
    return [
        jnp.sum(found[axis * rows : (axis + 1) * rows] * planes, axis=0, keepdims=True) for axis in range(3)
    ]


def weigh(weighted, planes, forces, cols, rows):
    for axis in range(3):
        high, low = split(planes * forces[axis])
        weighted[axis * rows : (axis + 1) * rows, cols] = high
        weighted[(3 + axis) * rows : (4 + axis) * rows, cols] = low


def contract(weighted, zcat):
    return lax.dot_general(weighted, zcat, (((1,), (1,)), ((), ())), preferred_element_type=F32)


def spread_at(spread, at, rows, total, fluid):
    result = []
    for axis in range(3):
        high, low = axis * total + at, (3 + axis) * total + at
        whole = spread[high : high + rows, 0:NZ] + spread[high : high + rows, NZ : 2 * NZ]
        result.append((whole + spread[low : low + rows, 0:NZ]) * fluid)
    return result


def moved(block, index, offset):
    _, shift_y, shift_z = DIRS[index]
    shift_y = (shift_y - offset) % block.shape[0]
    if shift_y:
        block = pltpu.roll(block, shift_y, 0)
    if shift_z:
        block = pltpu.roll(block, shift_z % NZ, 1)
    return block


def pack_kernel(own, solid, corner, frac, target, stiffness, disp, sent, bottom, top, block, walls, *held):
    sems = held[-1]
    held = held[:-1]
    small = [
        pltpu.make_async_copy(source, target_ref, sems.at[k])
        for k, (source, target_ref) in enumerate(zip((corner, frac, target, stiffness, disp), held))
    ]
    large = [
        pltpu.make_async_copy(solid, walls, sems.at[5]),
        pltpu.make_async_copy(own.at[:, :, ROWS - HALO :], bottom.at[0:19], sems.at[6]),
        pltpu.make_async_copy(own.at[:, :, :HALO], top.at[0:19], sems.at[7]),
    ]
    for copy in small + large:
        copy.start()
    for copy in small:
        copy.wait()
    corner, frac, target, stiffness, disp = held
    values = [corner[1:2].astype(F32), corner[2:3].astype(F32), frac[0:1], frac[1:2], frac[2:3], stiffness[...]]
    values += [target[axis : axis + 1] for axis in range(3)] + [disp[axis : axis + 1] for axis in range(3)]
    for r, value in enumerate(values):
        block[r // 2 : r // 2 + 1, 64 * (r % 2) : 64 * (r % 2) + 64] = value
    whole = block[0:6]
    peers = sent.shape[0]
    period = float(peers * ROWS)
    first = (lax.broadcasted_iota(jnp.int32, (6, LANES), 0) == 0) & (
        lax.broadcasted_iota(jnp.int32, (6, LANES), 1) < 64
    )
    for peer in range(peers):
        away = whole - float(peer * ROWS)
        away = away - jnp.where(away >= period / 2, period, jnp.where(away < -period / 2, -period, 0.0))
        sent[peer] = jnp.where(first, away, whole)
    for copy in large:
        copy.wait()
    for x in range(CX):
        wall = walls[x].astype(F32)
        bottom[19, x], top[19, x] = wall[ROWS - HALO :], wall[:HALO]


def relax_kernel(low, top, bottom, high, vcat, base, fluid, fluid_inner):
    for x in range(CX):
        wall = jnp.concatenate([part[19, x] for part in (low, top, bottom, high)], 0)
        is_fluid = 1.0 - wall
        fluid[x] = is_fluid
        fluid_inner[x] = pltpu.roll(is_fluid, EXT - TRIM, 0)[0:INNER]
        for half in range(2):
            rows = slice(half * 16, half * 16 + 16)

            def pop(i):
                before, after = (low, top) if half == 0 else (bottom, high)
                return jnp.concatenate([before[i, x], after[i, x]], 0)

            values = [pop(i) for i in range(19)]
            density, velocity = moments_of(values)
            for axis in range(3):
                at = axis * XY + x * EXT + half * 16
                vcat[at : at + 16, 0:NZ], vcat[at : at + 16, NZ : 2 * NZ] = split(velocity[axis])

            def put(i, value):
                base[i, x, rows] = value

            relaxed(values, density, velocity, is_fluid[rows] > 0.5, put)


def dense(cells, first, weights):
    offset = cells - first
    value = jnp.where(offset == 3.0, weights[3], 0.0)
    for k in (2, 1, 0):
        value = jnp.where(offset == float(k), weights[k], value)
    return value


def kernel_weights(frac):
    root = jnp.sqrt(1.0 + 4.0 * frac - 4.0 * frac * frac)
    second = (3.0 - 2.0 * frac + root) / 8.0
    third = (1.0 + 2.0 * frac + root) / 8.0
    return [0.5 - third, second, third, 0.5 - second]


def first_kernel(markers, vcat, base, fluid, post, up, down, zcat, state, xy, weighted, spread):
    left = lax.broadcasted_iota(jnp.int32, (6, LANES), 1) < 64
    z_cell = lax.broadcasted_iota(jnp.int32, (NZ, LANES), 0).astype(F32)
    y_cell = lax.broadcasted_iota(jnp.int32, (EXT, LANES), 0).astype(F32) - HALO
    for tile in range(16):
        cols = slice(tile * LANES, (tile + 1) * LANES)
        one, two = markers[2 * tile], markers[2 * tile + 1]
        even = jnp.where(left, one, pltpu.roll(two, 64, 1))
        odd = jnp.where(left, pltpu.roll(one, 64, 1), two)
        kx, ky, kz = kernel_weights(even[1:2]), kernel_weights(odd[1:2]), kernel_weights(even[2:3])
        zcat[0:NZ, cols], zcat[NZ : 2 * NZ, cols] = split(dense(z_cell, odd[0:1], kz))
        y_rows = dense(y_cell, even[0:1], ky)
        for x in range(CX):
            xy[x * EXT : (x + 1) * EXT, cols] = kx[x] * y_rows
        rows = (even[3:4], odd[3:4], even[4:5], odd[2:3], odd[4:5], even[5:6], odd[5:6], even[0:1], *kx, *ky)
        for r, value in enumerate(rows):
            state[r : r + 1, cols] = value

    for tile in range(8):
        cols = slice(tile * 256, (tile + 1) * 256)
        planes = xy[:, cols]
        forces = []
        for axis, mean in enumerate(interpolated(vcat[...], zcat, planes, cols, XY)):
            disp = state[4 + axis : 5 + axis, cols]
            forces.append(KAPPA * (state[axis : axis + 1, cols] - mean) - state[3:4, cols] * disp)
            state[4 + axis : 5 + axis, cols] = disp + mean
        weigh(weighted, planes, forces, cols, XY)
    spread[...] = contract(weighted[...], zcat[...])

    for x in range(CX):
        for tile in range(4):
            rows = slice(tile * 8, tile * 8 + 8)

            def put(i, value):
                post[i, x, rows] = value

            force = spread_at(spread, x * EXT + tile * 8, 8, XY, fluid[x, rows])
            forced(lambda i: base[i, x, rows], force, put)
    for j, index in enumerate(UP):
        up[j] = moved(post[index, CX - 1], index, TRIM)[0:INNER]
    for j, index in enumerate(DOWN):
        down[j] = moved(post[index, 0], index, TRIM)[0:INNER]


def relax_planes(plane_values, planes, fluid, base, velocities):
    for p, x in enumerate(planes):
        for tile in range(3):
            rows = slice(tile * 8, tile * 8 + 8)
            values = plane_values(x, rows)
            density, velocity = moments_of(values)
            for axis in range(3):
                at = (axis * 2 + p) * INNER + tile * 8
                velocities[at : at + 8, 0:NZ] = velocity[axis]

            def put(i, value):
                base[i, p, rows] = value

            relaxed(values, density, velocity, fluid[x, rows] > 0.5, put)


def inner_kernel(post, fluid, state, zcat, edge, base, found, xy, moving, velocities):
    for index in range(19):
        for x in range(CX):
            source = x - DIRS[index][0]
            if not 0 <= source < CX:
                continue
            plane = moved(post[index, source], index, TRIM)[0:INNER]
            if x in INSIDE:
                moving[index, x - 1] = plane
            else:
                edge[index, x // 3] = plane
    relax_planes(
        lambda x, rows: [moving[i, x - 1, rows] for i in range(19)], INSIDE, fluid, base, velocities
    )
    velocity = jnp.concatenate(split(velocities[...]), 1)
    y_cell = lax.broadcasted_iota(jnp.int32, (INNER, 256), 0).astype(F32) - (HALO - TRIM)
    for tile in range(8):
        cols = slice(tile * 256, (tile + 1) * 256)
        y_rows = dense(y_cell, state[7:8, cols], [state[12 + k : 13 + k, cols] for k in range(4)])
        for p, x in enumerate(INSIDE + OUTSIDE):
            xy[p * INNER : (p + 1) * INNER, cols] = state[8 + x : 9 + x, cols] * y_rows
        parts = interpolated(velocity, zcat, xy[0 : 2 * INNER, cols], cols, 2 * INNER)
        for axis in range(3):
            found[axis : axis + 1, cols] = parts[axis]


def second_kernel(edge, up, down, fluid, state, zcat, xy, found, base, force, back, velocities, moved_to):
    def plane_values(x, rows):
        def value(i):
            if x == 0 and DIRS[i][0] == 1:
                return up[UP.index(i), rows]
            if x == CX - 1 and DIRS[i][0] == -1:
                return down[DOWN.index(i), rows]
            return edge[i, x // 3, rows]

        return [value(i) for i in range(19)]

    relax_planes(plane_values, OUTSIDE, fluid, base, velocities)
    velocity = jnp.concatenate(split(velocities[...]), 1)
    left = lax.broadcasted_iota(jnp.int32, (1, LANES), 1) < 64
    for tile in range(8):
        cols = slice(tile * 256, (tile + 1) * 256)
        parts = interpolated(velocity, zcat, xy[2 * INNER : 4 * INNER, cols], cols, 2 * INNER)
        first = state[7:8, cols]
        mine = (first >= 0.0) & (first < float(ROWS))
        for axis in range(3):
            mean = found[axis : axis + 1, cols] + parts[axis]
            disp = state[4 + axis : 5 + axis, cols]
            pull = KAPPA * (state[axis : axis + 1, cols] - mean) - state[3:4, cols] * disp
            force[axis : axis + 1, cols] = pull
            moved_to[axis : axis + 1, cols] = jnp.where(mine, disp + mean, 0.0)
            moved_to[3 + axis : 4 + axis, cols] = jnp.where(mine, pull, 0.0)
    for tile in range(16):
        cols = slice(tile * LANES, (tile + 1) * LANES)
        for r in range(3):
            even, odd = moved_to[2 * r : 2 * r + 1, cols], moved_to[2 * r + 1 : 2 * r + 2, cols]
            back[2 * tile, r : r + 1] = jnp.where(left, even, pltpu.roll(odd, 64, 1))
            back[2 * tile + 1, r : r + 1] = jnp.where(left, pltpu.roll(even, 64, 1), odd)


def third_kernel(force, zcat, xy, fluid, inside, outside, post, up, down, weighted, spread):
    for tile in range(8):
        cols = slice(tile * 256, (tile + 1) * 256)
        forces = [force[axis : axis + 1, cols] for axis in range(3)]
        weigh(weighted, xy[:, cols], forces, cols, CX * INNER)
    spread[...] = contract(weighted[...], zcat[...])
    for p, x in enumerate(INSIDE + OUTSIDE):
        base = inside if p < 2 else outside
        for tile in range(3):
            rows = slice(tile * 8, tile * 8 + 8)

            def put(i, value):
                post[i, x, rows] = value

            push = spread_at(spread, p * INNER + tile * 8, 8, CX * INNER, fluid[x, rows])
            forced(lambda i: base[i, p % 2, rows], push, put)
    for j, index in enumerate(UP):
        up[j] = moved(post[index, CX - 1], index, HALO - TRIM)[0:ROWS]
    for j, index in enumerate(DOWN):
        down[j] = moved(post[index, 0], index, HALO - TRIM)[0:ROWS]


def stream_kernel(post, out):
    for index in range(19):
        for x in range(CX):
            source = x - DIRS[index][0]
            if 0 <= source < CX:
                out[index, x] = moved(post[index, source], index, HALO - TRIM)[0:ROWS]
            else:
                out[index, x] = jnp.zeros((ROWS, NZ), F32)


def fill_kernel(part, up, down, out, sems):
    copies = []
    for j, index in enumerate(UP):
        copies.append(pltpu.make_async_copy(up.at[j], out.at[index, 0], sems.at[j]))
    for j, index in enumerate(DOWN):
        copies.append(pltpu.make_async_copy(down.at[j], out.at[index, CX - 1], sems.at[5 + j]))
    for copy in copies:
        copy.start()
    for copy in copies:
        copy.wait()


IN_VMEM = pl.BlockSpec(memory_space=pltpu.VMEM)
ANYWHERE = pl.BlockSpec(memory_space=pl.ANY)


def near(x):
    return pltpu.with_memory_space_constraint(x, pltpu.VMEM)


def run(kernel, args, outs, scratch=(), cost=4_000_000):
    return pl.pallas_call(
        kernel,
        out_shape=outs,
        in_specs=[IN_VMEM] * len(args),
        out_specs=jax.tree.map(lambda _: IN_VMEM, outs, is_leaf=lambda leaf: not isinstance(leaf, tuple)),
        scratch_shapes=list(scratch),
        compiler_params=pltpu.CompilerParams(vmem_limit_bytes=24 * 2**20),
        cost_estimate=pl.CostEstimate(flops=0, transcendentals=0, bytes_accessed=cost),
    )(*args)


def ring(axis):
    peers = lax.axis_size(axis)
    forward = [(i, (i + 1) % peers) for i in range(peers)]
    return forward, [(j, i) for i, j in forward]


def parts(populations, solid, marker_corner, marker_frac, marker_target, stiffness, displacement):
    peers = lax.axis_size("sub")
    sub_up, sub_down = ring("sub")
    plate_up, plate_down = ring("plate")
    args = (populations, solid, marker_corner, marker_frac, marker_target, stiffness.reshape(1, 64), displacement)
    shape = (20, CX, HALO, NZ)
    sent, bottom, top = pl.pallas_call(
        pack_kernel,
        out_shape=(
            jax.ShapeDtypeStruct((peers, 6, LANES), F32),
            pltpu.VMEM(shape, F32),
            pltpu.VMEM(shape, F32),
        ),
        in_specs=[pl.BlockSpec(memory_space=pltpu.HBM)] * 7,
        out_specs=[IN_VMEM] * 3,
        scratch_shapes=[
            pltpu.VMEM((8, LANES), F32),
            pltpu.VMEM(solid.shape, jnp.int32),
            *[pltpu.VMEM(arg.shape, arg.dtype) for arg in args[2:]],
            pltpu.SemaphoreType.DMA((8,)),
        ],
        compiler_params=pltpu.CompilerParams(vmem_limit_bytes=8 * 2**20),
        name="pack_kernel",
    )(*[pltpu.with_memory_space_constraint(arg, pltpu.HBM) for arg in args])
    markers = lax.all_to_all(sent, "sub", 0, 0, tiled=True)
    low = lax.ppermute(bottom, "sub", sub_up)
    high = lax.ppermute(top, "sub", sub_down)
    vcat, base, fluid, fluid_inner = run(
        relax_kernel,
        (near(low), near(top), near(bottom), near(high)),
        (
            pltpu.VMEM((3 * XY, 2 * NZ), BF16),
            pltpu.VMEM((19, CX, EXT, NZ), F32),
            pltpu.VMEM((CX, EXT, NZ), F32),
            pltpu.VMEM((CX, INNER, NZ), F32),
        ),
    )
    post, up, down, zcat, state = run(
        first_kernel,
        (near(markers), near(vcat), near(base), near(fluid)),
        (
            pltpu.VMEM((19, CX, EXT, NZ), F32),
            pltpu.VMEM((5, INNER, NZ), F32),
            pltpu.VMEM((5, INNER, NZ), F32),
            pltpu.VMEM((2 * NZ, MARKERS), BF16),
            pltpu.VMEM((16, MARKERS), F32),
        ),
        (
            pltpu.VMEM((XY, MARKERS), F32),
            pltpu.VMEM((6 * XY, MARKERS), BF16),
            pltpu.VMEM((6 * XY, 2 * NZ), F32),
        ),
    )
    up = lax.ppermute(up, "plate", plate_up)
    down = lax.ppermute(down, "plate", plate_down)
    edge, inside, found, xy = run(
        inner_kernel,
        (near(post), near(fluid_inner), near(state), near(zcat)),
        (
            pltpu.VMEM((19, 2, INNER, NZ), F32),
            pltpu.VMEM((19, 2, INNER, NZ), F32),
            pltpu.VMEM((8, MARKERS), F32),
            pltpu.VMEM((CX * INNER, MARKERS), F32),
        ),
        (pltpu.VMEM((19, 2, INNER, NZ), F32), pltpu.VMEM((6 * INNER, NZ), F32)),
        cost=12_000_000,
    )
    outside, force, back = run(
        second_kernel,
        (near(edge), near(up), near(down), near(fluid_inner), near(state), near(zcat), near(xy), near(found)),
        (
            pltpu.VMEM((19, 2, INNER, NZ), F32),
            pltpu.VMEM((8, MARKERS), F32),
            jax.ShapeDtypeStruct((peers, 3, LANES), F32),
        ),
        (pltpu.VMEM((6 * INNER, NZ), F32), pltpu.VMEM((8, MARKERS), F32)),
    )
    back = lax.all_to_all(back, "sub", 0, 0, tiled=True)
    post, up, down = run(
        third_kernel,
        (near(force), near(zcat), near(xy), near(fluid_inner), near(inside), near(outside)),
        (
            pltpu.VMEM((19, CX, INNER, NZ), F32),
            pltpu.VMEM((5, ROWS, NZ), F32),
            pltpu.VMEM((5, ROWS, NZ), F32),
        ),
        (pltpu.VMEM((6 * CX * INNER, MARKERS), BF16), pltpu.VMEM((6 * CX * INNER, 2 * NZ), F32)),
    )
    up = lax.ppermute(up, "plate", plate_up)
    down = lax.ppermute(down, "plate", plate_down)
    part = run(stream_kernel, (near(post),), jax.ShapeDtypeStruct((19, CX, ROWS, NZ), F32))
    out = pl.pallas_call(
        fill_kernel,
        out_shape=jax.ShapeDtypeStruct((19, CX, ROWS, NZ), F32),
        in_specs=[ANYWHERE, IN_VMEM, IN_VMEM],
        out_specs=ANYWHERE,
        scratch_shapes=[pltpu.SemaphoreType.DMA((10,))],
        input_output_aliases={0: 0},
        compiler_params=pltpu.CompilerParams(vmem_limit_bytes=8 * 2**20),
        name="fill_kernel",
    )(part, near(up), near(down))
    result = jnp.sum(back, 0).reshape(6, 64)
    return (out, result[:3], result[3:])


def solution(mesh):
    in_specs = (
        P(None, "plate", "sub", None),
        P("plate", "sub", None),
        P(None, ("plate", "sub")),
        P(None, ("plate", "sub")),
        P(None, ("plate", "sub")),
        P(("plate", "sub")),
        P(None, ("plate", "sub")),
    )
    out_specs = (
        P(None, "plate", "sub", None),
        P(None, ("plate", "sub")),
        P(None, ("plate", "sub")),
    )
    return jax.shard_map(parts, mesh=mesh, in_specs=in_specs, out_specs=out_specs, check_vma=False)
```

time: 459 us -> 54.9 us (0.12)
  waiting for transfers between devices: 244 us -> 18.6 us
  blocking collectives: 160 us -> 0 us
  between operations: 14.7 us -> 0.71 us
  Pallas kernels: 0 us -> 9.76 us
  matrix products: 7.68 us -> 0 us
  starting transfers between devices: 16.9 us -> 24.1 us
  other arithmetic: 6.96 us -> 0.04 us
  local copies, waits for them, and re-layouts: 7.34 us -> 0.67 us
    unnamed x4 -> x0, waiting for transfers between devices: 226 us -> none
    all_gather x4 -> x0, blocking collectives: 160 us -> none  [the longest x2 78.3 us: shards(): plate_force = lax.all_gather(force, 'sub', axis=1, tiled=True)]
    ppermute x8 -> x6, waiting for transfers between devices: 18.7 us -> 4.69 us  [the longest x2 2.82 us: parts(): up = lax.ppermute(up, 'plate', plate_up)]
    all_to_all x0 -> x2, waiting for transfers between devices: none -> 13.9 us  [the longest x1 11.4 us: parts(): markers = lax.all_to_all(sent, 'sub', 0, 0, tiled=True)]
    all_to_all x0 -> x2, starting transfers between devices: none -> 10.3 us  [the longest x1 6.43 us: parts(): markers = lax.all_to_all(sent, 'sub', 0, 0, tiled=True)]
    pallas_call x0 -> x8, Pallas kernels: none -> 9.76 us  [the longest x6 7.15 us: run(): pl.pallas_call(kernel, out_shape=outs, in_specs=[IN_VMEM] * len(args), ou...]
    dot_general x4 -> x0, matrix products: 7.68 us -> none  [the longest x2 3.84 us: shards(): jnp.einsum('kcz,zm->kcm', flat, z_rows, precision=lax.Precision.HIGHEST)]
    unnamed x28 -> x0, local copies, waits for them, and re-layouts: 5.71 us -> none
  transfers between devices with their start and end apart: 10 -> 8, of which waited for: 8 -> 6; matrix products, arithmetic and copies ran while one was open for 0% -> 0% of each run, Pallas kernels for 0% -> 7%
where the time goes in v1:
time: 54.9 us; the launch traced here: 53.9 us
  starting transfers between devices  24.1 us (44%)
  waiting for transfers between devices  18.6 us (34%)
  Pallas kernels  9.76 us (18%)
  between operations  0.71 us (1%)
  local copies, waits for them, and re-layouts  0.67 us (1%)
    all_to_all x1, waiting for transfers between devices, parts(): markers = lax.all_to_all(sent, 'sub', 0, 0, tiled=True)  11.4 us
    ppermute x1, starting transfers between devices, parts(): high = lax.ppermute(top, 'sub', sub_down)  7.83 us
    pallas_call x6, Pallas kernels, run(): pl.pallas_call(kernel, out_shape=outs, in_specs=[IN_VMEM] * len(args), ou...  7.15 us
    all_to_all x1, starting transfers between devices, parts(): markers = lax.all_to_all(sent, 'sub', 0, 0, tiled=True)  6.43 us
    all_to_all x1, starting transfers between devices, parts(): back = lax.all_to_all(back, 'sub', 0, 0, tiled=True)  3.84 us
    ppermute x2, starting transfers between devices, parts(): down = lax.ppermute(down, 'plate', plate_down)  3 us
    ppermute x2, starting transfers between devices, parts(): up = lax.ppermute(up, 'plate', plate_up)  2.93 us
    ppermute x2, waiting for transfers between devices, parts(): up = lax.ppermute(up, 'plate', plate_up)  2.82 us
  transfers between devices with their start and end apart: 8, of which 6 were waited for; matrix products, arithmetic and copies ran while one was open for 0% of the time, Pallas kernels for 7%

profile of v1, /device:TPU:8, one launch (start us, length us, event | category | flops | bytes accessed | tf_op | source)
XLA Modules:
  0.0 53.9 jit_solution(653820798013073054)
XLA Ops:
  0.6 1.9 %pack_kernel.1 = (f32[32,6,128]{2,1,0:T(8,128)}, f32[20,4,8,128]{3,2,1,0:T(8,128)S(1)}, f32[20,4,8,128]{3,2,1,0:T(8,128)S(1)}) custom-call(f32[19,4,16,128]{3,2,1,0:T(8,128)} %own.1, s32[4,16,128]{2,1,0:T(8,128)} %solid.1, s32[3,64]{1,0:T(4,128)} %corner.1, f32[3,64]{1,0:T(4,128)} %frac.1, f32[3,64]{1,0:T(4,128)} %target.1, f32[1,64]{1,0:T(1,128)} %bitcast.1, ...), custom_call_target="tpu_custom_call" | custom-call | tf_op jit(solution)/shard_map/pack_kernel/pallas_call | solution.py:420
  2.5 0.1 collective-permute-start
  2.6 7.8 %collective-permute-start.1 = (f32[20,4,8,128]{3,2,1,0:T(8,128)S(1)}, f32[20,4,8,128]{3,2,1,0:T(8,128)S(1)}, u32[]{:S(2)}, u32[]{:S(2)}) collective-permute-start(f32[20,4,8,128]{3,2,1,0:T(8,128)S(1)} %get-tuple-element.27.top), channel_id=1, source_target_pairs={{1,0},{2,1},{3,2},{4,3},{5,4},{6,5},{7,6},{8,7},{9,8},{10,9},{11,1... | collective-permute-start | bytes 983048 | tf_op jit(solution)/shard_map/ppermute | solution.py:440
  10.4 6.4 %all-to-all-start = ((f32[32,6,128]{2,1,0:T(8,128)}), f32[32,6,128]{2,1,0:T(8,128)S(1)}, u32[]{:S(2)}, u32[]{:S(2)}) async-start(f32[32,6,128]{2,1,0:T(8,128)} %get-tuple-element.25), calls=%async_computation | async-start | bytes 262144 | tf_op jit(solution)/shard_map/all_to_all | solution.py:438
  16.9 0.0 collective-permute-done.low
  16.9 0.0 collective-permute-done.1.high
  16.9 0.5 shard_map.94
  17.4 11.4 %all-to-all-done.markers = f32[32,6,128]{2,1,0:T(8,128)S(1)} async-done(((f32[32,6,128]{2,1,0:T(8,128)}), f32[32,6,128]{2,1,0:T(8,128)S(1)}, u32[]{:S(2)}, u32[]{:S(2)}) %all-to-all-start) | async-done | bytes 98336 | tf_op jit(solution)/shard_map/all_to_all | solution.py:438
  28.8 2.6 %shard_map.95 = (f32[19,4,32,128]{3,2,1,0:T(8,128)S(1)}, f32[5,24,128]{2,1,0:T(8,128)S(1)}, f32[5,24,128]{2,1,0:T(8,128)S(1)}, bf16[256,2048]{1,0:T(8,128)(2,1)S(1)}, f32[16,2048]{1,0:T(8,128)S(1)}) custom-call(f32[32,6,128]{2,1,0:T(8,128)S(1)} %all-to-all-done.markers, bf16[384,256]{1,0:T(8,128)(2,1)S(1)} %get-tuple-element.28.vcat, ...), custom_call_target="tpu_custom_call" | custom-call | bytes 4000000 | tf_op jit(solution)/shard_map/pallas_call | solution.py:397
  31.5 0.6 %collective-permute-start.2 = (f32[5,24,128]{2,1,0:T(8,128)S(1)}, f32[5,24,128]{2,1,0:T(8,128)S(1)}, u32[]{:S(2)}, u32[]{:S(2)}) collective-permute-start(f32[5,24,128]{2,1,0:T(8,128)S(1)} %get-tuple-element.36), channel_id=1, source_target_pairs={{0,32},{32,64},{64,96},{96,128},{128,160},{160,192},{192,224},{224... | collective-permute-start | bytes 184328 | tf_op jit(solution)/shard_map/ppermute | solution.py:467
  32.1 2.3 %collective-permute-start.3 = (f32[5,24,128]{2,1,0:T(8,128)S(1)}, f32[5,24,128]{2,1,0:T(8,128)S(1)}, u32[]{:S(2)}, u32[]{:S(2)}) collective-permute-start(f32[5,24,128]{2,1,0:T(8,128)S(1)} %get-tuple-element.37), channel_id=1, source_target_pairs={{32,0},{64,32},{96,64},{128,96},{160,128},{192,160},{224,192},{0,2... | collective-permute-start | bytes 184328 | tf_op jit(solution)/shard_map/ppermute | solution.py:468
  34.4 0.7 %shard_map.96 = (f32[19,2,24,128]{3,2,1,0:T(8,128)S(1)}, f32[19,2,24,128]{3,2,1,0:T(8,128)S(1)}, f32[8,2048]{1,0:T(8,128)S(1)}, f32[96,2048]{1,0:T(8,128)S(1)}) custom-call(f32[19,4,32,128]{3,2,1,0:T(8,128)S(1)} %get-tuple-element.31.post, f32[4,24,128]{2,1,0:T(8,128)S(1)} %get-tuple-element.32.fluid, f32[16,2048]{1,0:T(8,128)S(1)} %get-tuple-element.33.state, ...), custom_call_target="tpu_custom_call" | custom-call | bytes 12000000 | tf_op jit(solution)/shard_map/pallas_call | solution.py:397
  35.1 1.5 %collective-permute-done.2.up = f32[5,24,128]{2,1,0:T(8,128)S(1)} collective-permute-done((f32[5,24,128]{2,1,0:T(8,128)S(1)}, f32[5,24,128]{2,1,0:T(8,128)S(1)}, u32[]{:S(2)}, u32[]{:S(2)}) %collective-permute-start.2) | collective-permute-done | bytes 61472 | tf_op jit(solution)/shard_map/ppermute | solution.py:467
  36.6 0.8 %collective-permute-done.3.down = f32[5,24,128]{2,1,0:T(8,128)S(1)} collective-permute-done((f32[5,24,128]{2,1,0:T(8,128)S(1)}, f32[5,24,128]{2,1,0:T(8,128)S(1)}, u32[]{:S(2)}, u32[]{:S(2)}) %collective-permute-start.3) | collective-permute-done | bytes 61472 | tf_op jit(solution)/shard_map/ppermute | solution.py:468
  37.4 1.4 %shard_map.97 = (f32[19,2,24,128]{3,2,1,0:T(8,128)S(1)}, f32[8,2048]{1,0:T(8,128)S(1)}, f32[32,3,128]{2,1,0:T(4,128)}) custom-call(f32[19,2,24,128]{3,2,1,0:T(8,128)S(1)} %get-tuple-element.35.edge, f32[5,24,128]{2,1,0:T(8,128)S(1)} %collective-permute-done.2.up, f32[5,24,128]{2,1,0:T(8,128)S(1)} %collective-permute-done.3.down, ...), custom_call_target="tpu_custom_call" | custom-call | bytes 4000000 | tf_op jit(solution)/shard_map/pallas_call | solution.py:397
  38.8 3.8 %all-to-all-start.1 = ((f32[32,3,128]{2,1,0:T(4,128)}), f32[32,3,128]{2,1,0:T(4,128)S(1)}, u32[]{:S(2)}, u32[]{:S(2)}) async-start(f32[32,3,128]{2,1,0:T(4,128)} %get-tuple-element.46), calls=%async_computation.1 | async-start | bytes 131072 | tf_op jit(solution)/shard_map/all_to_all | solution.py:491
  42.6 0.9 %shard_map.98 = (f32[19,4,24,128]{3,2,1,0:T(8,128)S(1)}, f32[5,16,128]{2,1,0:T(8,128)S(1)}, f32[5,16,128]{2,1,0:T(8,128)S(1)}) custom-call(f32[8,2048]{1,0:T(8,128)S(1)} %get-tuple-element.40.force, bf16[256,2048]{1,0:T(8,128)(2,1)S(1)} %get-tuple-element.34.zcat, f32[96,2048]{1,0:T(8,128)S(1)} %get-tuple-element.38.xy, ...), custom_call_target="tpu_custom_call" | custom-call | bytes 4000000 | tf_op jit(solution)/shard_map/pallas_call | solution.py:397
  43.6 2.3 %collective-permute-start.4 = (f32[5,16,128]{2,1,0:T(8,128)S(1)}, f32[5,16,128]{2,1,0:T(8,128)S(1)}, u32[]{:S(2)}, u32[]{:S(2)}) collective-permute-start(f32[5,16,128]{2,1,0:T(8,128)S(1)} %get-tuple-element.44), channel_id=1, source_target_pairs={{0,32},{32,64},{64,96},{96,128},{128,160},{160,192},{192,224},{224... | collective-permute-start | bytes 122888 | tf_op jit(solution)/shard_map/ppermute | solution.py:502
  45.8 0.7 %collective-permute-start.5 = (f32[5,16,128]{2,1,0:T(8,128)S(1)}, f32[5,16,128]{2,1,0:T(8,128)S(1)}, u32[]{:S(2)}, u32[]{:S(2)}) collective-permute-start(f32[5,16,128]{2,1,0:T(8,128)S(1)} %get-tuple-element.45), channel_id=1, source_target_pairs={{32,0},{64,32},{96,64},{128,96},{160,128},{192,160},{224,192},{0,2... | collective-permute-start | bytes 122888 | tf_op jit(solution)/shard_map/ppermute | solution.py:503
  46.5 1.0 %shard_map.99.part = f32[19,4,16,128]{3,2,1,0:T(8,128)} custom-call(f32[19,4,24,128]{3,2,1,0:T(8,128)S(1)} %get-tuple-element.43.post), custom_call_target="tpu_custom_call" | custom-call | bytes 4000000 | tf_op jit(solution)/shard_map/pallas_call | solution.py:397
  47.5 1.4 %collective-permute-done.4.up = f32[5,16,128]{2,1,0:T(8,128)S(1)} collective-permute-done((f32[5,16,128]{2,1,0:T(8,128)S(1)}, f32[5,16,128]{2,1,0:T(8,128)S(1)}, u32[]{:S(2)}, u32[]{:S(2)}) %collective-permute-start.4) | collective-permute-done | bytes 40992 | tf_op jit(solution)/shard_map/ppermute | solution.py:502
  48.8 1.1 %collective-permute-done.5.down = f32[5,16,128]{2,1,0:T(8,128)S(1)} collective-permute-done((f32[5,16,128]{2,1,0:T(8,128)S(1)}, f32[5,16,128]{2,1,0:T(8,128)S(1)}, u32[]{:S(2)}, u32[]{:S(2)}) %collective-permute-start.5) | collective-permute-done | bytes 40992 | tf_op jit(solution)/shard_map/ppermute | solution.py:503
  49.9 0.7 %fill_kernel.1 = f32[19,4,16,128]{3,2,1,0:T(8,128)} custom-call(f32[19,4,16,128]{3,2,1,0:T(8,128)} %shard_map.99.part, f32[5,16,128]{2,1,0:T(8,128)S(1)} %collective-permute-done.4.up, f32[5,16,128]{2,1,0:T(8,128)S(1)} %collective-permute-done.5.down), custom_call_target="tpu_custom_call", output_to_operand_aliasing={{}: (0, {})} | custom-call | tf_op jit(solution)/shard_map/fill_kernel/pallas_call | solution.py:505
  50.6 2.5 %all-to-all-done.1 = f32[32,3,128]{2,1,0:T(4,128)S(1)} async-done(((f32[32,3,128]{2,1,0:T(4,128)}), f32[32,3,128]{2,1,0:T(4,128)S(1)}, u32[]{:S(2)}, u32[]{:S(2)}) %all-to-all-start.1) | async-done | bytes 49184 | tf_op jit(solution)/shard_map/all_to_all | solution.py:491
  53.2 0.1 reshape.13
  53.3 0.6 %fusion = (f32[3,64]{1,0:T(4,128)}, f32[3,64]{1,0:T(4,128)}) fusion(f32[6,64]{1,0:T(8,128)S(1)} %reshape.13), kind=kLoop, calls=%fused_computation | loop fusion | bytes 3072 | tf_op jit(solution)/shard_map/slice | solution.py:516
  (1 shorter events, 0.0 us)
Async XLA Ops:
  2.5 14.4 %collective-permute-start = (f32[20,4,8,128]{3,2,1,0:T(8,128)S(1)}, f32[20,4,8,128]{3,2,1,0:T(8,128)S(1)}, u32[]{:S(2)}, u32[]{:S(2)}) collective-permute-start(f32[20,4,8,128]{3,2,1,0:T(8,128)S(1)} %get-tuple-element.26.bottom), channel_id=1, source_target_pairs={{0,1},{1,2},{2,3},{3,4},{4,5},{5,6},{6,7},{7,8},{8,9},{9,10},{10,1... | collective-permute-start | bytes 983048 | tf_op jit(solution)/shard_map/ppermute | solution.py:439
  2.6 14.3 %collective-permute-start.1 = (f32[20,4,8,128]{3,2,1,0:T(8,128)S(1)}, f32[20,4,8,128]{3,2,1,0:T(8,128)S(1)}, u32[]{:S(2)}, u32[]{:S(2)}) collective-permute-start(f32[20,4,8,128]{3,2,1,0:T(8,128)S(1)} %get-tuple-element.27.top), channel_id=1, source_target_pairs={{1,0},{2,1},{3,2},{4,3},{5,4},{6,5},{7,6},{8,7},{9,8},{10,9},{11,1... | collective-permute-start | bytes 983048 | tf_op jit(solution)/shard_map/ppermute | solution.py:440
  10.4 18.4 %all-to-all-start = ((f32[32,6,128]{2,1,0:T(8,128)}), f32[32,6,128]{2,1,0:T(8,128)S(1)}, u32[]{:S(2)}, u32[]{:S(2)}) async-start(f32[32,6,128]{2,1,0:T(8,128)} %get-tuple-element.25), calls=%async_computation | async-start | bytes 262144 | tf_op jit(solution)/shard_map/all_to_all | solution.py:438
  31.5 5.2 %collective-permute-start.2 = (f32[5,24,128]{2,1,0:T(8,128)S(1)}, f32[5,24,128]{2,1,0:T(8,128)S(1)}, u32[]{:S(2)}, u32[]{:S(2)}) collective-permute-start(f32[5,24,128]{2,1,0:T(8,128)S(1)} %get-tuple-element.36), channel_id=1, source_target_pairs={{0,32},{32,64},{64,96},{96,128},{128,160},{160,192},{192,224},{224... | collective-permute-start | bytes 184328 | tf_op jit(solution)/shard_map/ppermute | solution.py:467
  32.1 5.3 %collective-permute-start.3 = (f32[5,24,128]{2,1,0:T(8,128)S(1)}, f32[5,24,128]{2,1,0:T(8,128)S(1)}, u32[]{:S(2)}, u32[]{:S(2)}) collective-permute-start(f32[5,24,128]{2,1,0:T(8,128)S(1)} %get-tuple-element.37), channel_id=1, source_target_pairs={{32,0},{64,32},{96,64},{128,96},{160,128},{192,160},{224,192},{0,2... | collective-permute-start | bytes 184328 | tf_op jit(solution)/shard_map/ppermute | solution.py:468
  38.8 14.4 %all-to-all-start.1 = ((f32[32,3,128]{2,1,0:T(4,128)}), f32[32,3,128]{2,1,0:T(4,128)S(1)}, u32[]{:S(2)}, u32[]{:S(2)}) async-start(f32[32,3,128]{2,1,0:T(4,128)} %get-tuple-element.46), calls=%async_computation.1 | async-start | bytes 131072 | tf_op jit(solution)/shard_map/all_to_all | solution.py:491
  43.6 5.3 %collective-permute-start.4 = (f32[5,16,128]{2,1,0:T(8,128)S(1)}, f32[5,16,128]{2,1,0:T(8,128)S(1)}, u32[]{:S(2)}, u32[]{:S(2)}) collective-permute-start(f32[5,16,128]{2,1,0:T(8,128)S(1)} %get-tuple-element.44), channel_id=1, source_target_pairs={{0,32},{32,64},{64,96},{96,128},{128,160},{160,192},{192,224},{224... | collective-permute-start | bytes 122888 | tf_op jit(solution)/shard_map/ppermute | solution.py:502
  45.8 4.1 %collective-permute-start.5 = (f32[5,16,128]{2,1,0:T(8,128)S(1)}, f32[5,16,128]{2,1,0:T(8,128)S(1)}, u32[]{:S(2)}, u32[]{:S(2)}) collective-permute-start(f32[5,16,128]{2,1,0:T(8,128)S(1)} %get-tuple-element.45), channel_id=1, source_target_pairs={{32,0},{64,32},{96,64},{128,96},{160,128},{192,160},{224,192},{0,2... | collective-permute-start | bytes 122888 | tf_op jit(solution)/shard_map/ppermute | solution.py:503

commit v2 on v1

v2 whole, which is shorter than its diff:
```python
import functools
import jax
import jax.numpy as jnp
from jax import lax
from jax.experimental import pallas as pl
from jax.experimental.pallas import tpu as pltpu
from jax.sharding import PartitionSpec as P

DIRS = [
    (0, 0, 0),
    (1, 0, 0),
    (-1, 0, 0),
    (0, 1, 0),
    (0, -1, 0),
    (0, 0, 1),
    (0, 0, -1),
    (1, 1, 0),
    (-1, -1, 0),
    (1, -1, 0),
    (-1, 1, 0),
    (1, 0, 1),
    (-1, 0, -1),
    (1, 0, -1),
    (-1, 0, 1),
    (0, 1, 1),
    (0, -1, -1),
    (0, 1, -1),
    (0, -1, 1),
]
WEIGHTS = [1.0 / 3.0] + [1.0 / 18.0] * 6 + [1.0 / 36.0] * 12
KAPPA = 4.0
RELAX = 0.9
UP = [i for i in range(19) if DIRS[i][0] == 1]
DOWN = [i for i in range(19) if DIRS[i][0] == -1]

CX = 4
ROWS = 16
HALO = 8
EXT = ROWS + 2 * HALO
NZ = 128
XY = CX * EXT
TRIM = 4
INNER = EXT - 2 * TRIM
MARKERS = 2048
VEL, FULL = 3, 5
AT_VEL, AT_PLANE = 8, 48
SENT_ROWS = AT_PLANE + 20 * CX * FULL + 8
KX, FORCE, STATE = 8, 12, 15
KY, KZ, WORK = 4, 8, 12
INSIDE, OUTSIDE = (1, 2), (0, 3)
LANES = 128
F32 = jnp.float32
BF16 = jnp.bfloat16


def split(value):
    high = value.astype(BF16)
    low = (value - high.astype(F32)).astype(BF16)
    return high, low


def moments_of(values):
    density = functools.reduce(lambda a, b: a + b, values)
    inverse = 1.0 / density
    velocity = []
    for axis in range(3):
        plus = functools.reduce(lambda a, b: a + b, [values[i] for i in range(19) if DIRS[i][axis] == 1])
        minus = functools.reduce(lambda a, b: a + b, [values[i] for i in range(19) if DIRS[i][axis] == -1])
        velocity.append((plus - minus) * inverse)
    return density, velocity


def along(index, vectors):
    total = None
    for axis in range(3):
        sign = DIRS[index][axis]
        if sign == 0:
            continue
        if total is None:
            total = vectors[axis] if sign == 1 else -vectors[axis]
        else:
            total = total + vectors[axis] if sign == 1 else total - vectors[axis]
    return total


def relaxed(values, density, velocity, fluid, put, indices=range(19)):
    keep, rate = 1.0 - 1.0 / RELAX, 1.0 / RELAX
    scaled = density * rate
    base = scaled - 1.5 * scaled * (
        velocity[0] * velocity[0] + velocity[1] * velocity[1] + velocity[2] * velocity[2]
    )
    if 0 in indices:
        put(0, jnp.where(fluid, keep * values[0] + WEIGHTS[0] * base, values[0]))
    for index in range(1, 19, 2):
        if index not in indices:
            continue
        weight = WEIGHTS[index]
        first, second = values[index], values[index + 1]
        proj = along(index, velocity)
        scaled_proj = scaled * proj
        even = weight * (base + 4.5 * scaled_proj * proj)
        odd = (3.0 * weight) * scaled_proj
        put(index, jnp.where(fluid, keep * first + (even + odd), second))
        put(index + 1, jnp.where(fluid, keep * second + (even - odd), first))


def forced(base, force, put, indices=range(19)):
    if 0 in indices:
        put(0, base(0))
    for index in range(1, 19, 2):
        if index not in indices:
            continue
        push = (3.0 * WEIGHTS[index]) * along(index, force)
        put(index, base(index) + push)
        put(index + 1, base(index + 1) - push)


def interpolated(velocity, zcat, cols):
    z_high, z_low = zcat[0:NZ, cols], zcat[NZ : 2 * NZ, cols]
    return jnp.dot(velocity, jnp.concatenate([z_high, z_high, z_low], 0), preferred_element_type=F32)


def tripled(velocity):
    high, low = split(velocity)
    return jnp.concatenate([high, low, high], 1)


def averaged(found, y_rows, kx):
    rows = y_rows.shape[0]
    total = None
    for p, weight in enumerate(kx):
        product = found[p * rows : (p + 1) * rows] * y_rows
        part = sum(product[t * 8 + 8 : t * 8 + 16] for t in range(rows // 8 - 1)) + product[0:8]
        total = part * weight if total is None else total + part * weight
    return jnp.sum(total, axis=0, keepdims=True)


def weigh(weighted, ys, forces, state, planes, rows):
    for tile in range(16):
        cols = slice(tile * LANES, (tile + 1) * LANES)
        y_rows = ys[:, cols]
        for axis in range(3):
            for p, x in enumerate(planes):
                scale = forces(axis, tile) * state[KX + x, tile : tile + 1]
                at = (axis * 2 + p) * rows
                high, low = split(y_rows * scale)
                weighted[at : at + rows, cols] = high
                weighted[6 * rows + at : 6 * rows + at + rows, cols] = low


def contract(weighted, zcat):
    return lax.dot_general(weighted, zcat, (((1,), (1,)), ((), ())), preferred_element_type=F32)


def spread_at(spread, p, tile, rows, fluid):
    result = []
    for axis in range(3):
        at = (axis * 2 + p) * rows + tile * 8
        low = 6 * rows + at
        whole = spread[at : at + 8, 0:NZ] + spread[at : at + 8, NZ : 2 * NZ]
        result.append((whole + spread[low : low + 8, 0:NZ]) * fluid)
    return result


def moved(block, index, offset):
    _, shift_y, shift_z = DIRS[index]
    shift_y = (shift_y - offset) % block.shape[0]
    if shift_y:
        block = pltpu.roll(block, shift_y, 0)
    if shift_z:
        block = pltpu.roll(block, shift_z % NZ, 1)
    return block


def pack_kernel(own, solid, corner, frac, target, stiffness, disp, sent, cells, bottom, top, block, walls, *held):
    sems = held[-1]
    held = held[:-1]
    small = [
        pltpu.make_async_copy(source, target_ref, sems.at[k])
        for k, (source, target_ref) in enumerate(zip((corner, frac, target, stiffness, disp), held))
    ]
    large = [
        pltpu.make_async_copy(solid, walls, sems.at[5]),
        pltpu.make_async_copy(own, cells.at[0:19], sems.at[6]),
    ]
    for copy in small + large:
        copy.start()
    for copy in small:
        copy.wait()
    corner, frac, target, stiffness, disp = held
    values = [corner[1:2].astype(F32), corner[2:3].astype(F32), frac[0:1], frac[1:2], frac[2:3], stiffness[...]]
    values += [target[axis : axis + 1] for axis in range(3)] + [disp[axis : axis + 1] for axis in range(3)]
    for r, value in enumerate(values):
        block[r // 2 : r // 2 + 1, 64 * (r % 2) : 64 * (r % 2) + 64] = value
    whole = block[0:6]
    peers = sent.shape[0]
    period = float(peers * ROWS)
    first = (lax.broadcasted_iota(jnp.int32, (6, LANES), 0) == 0) & (
        lax.broadcasted_iota(jnp.int32, (6, LANES), 1) < 64
    )
    for peer in range(peers):
        away = whole - float(peer * ROWS)
        away = away - jnp.where(away >= period / 2, period, jnp.where(away < -period / 2, -period, 0.0))
        sent[peer] = jnp.where(first, away, whole)
    for copy in large:
        copy.wait()
    for buffer in (bottom, top):
        for at in (0, AT_PLANE - 8, SENT_ROWS - 8):
            buffer[at : at + 8] = jnp.zeros((8, NZ), F32)
    for x in range(CX):
        cells[19, x] = walls[x].astype(F32)
        for buffer, rows, full, vel in ((bottom, slice(8, 16), 3, 0), (top, slice(0, 8), 0, 5)):
            values = [cells[i, x, rows] for i in range(20)]
            for i, value in enumerate(values):
                at = AT_PLANE + (i * CX + x) * FULL
                buffer[at : at + FULL] = value[full : full + FULL]
            for axis, value in enumerate(moments_of(values[0:19])[1]):
                at = AT_VEL + (axis * CX + x) * VEL
                buffer[at : at + VEL] = value[vel : vel + VEL]


def relax_kernel(low, cells, high, vcat, base, fluid, fluid_inner):
    row = lax.broadcasted_iota(jnp.int32, (8, NZ), 0)
    for x in range(CX):

        def before(i):
            at = AT_PLANE + (i * CX + x) * FULL - VEL
            return low[at : at + 8]

        def after(i):
            at = AT_PLANE + (i * CX + x) * FULL
            return high[at : at + 8]

        wall = jnp.concatenate([before(19), cells[19, x], after(19)], 0)
        is_fluid = 1.0 - wall
        fluid[x] = is_fluid
        fluid_inner[x] = pltpu.roll(is_fluid, EXT - TRIM, 0)[0:INNER]
        for half in range(2):
            rows = slice(half * 16, half * 16 + 16)

            def pop(i):
                if half == 0:
                    return jnp.concatenate([before(i), cells[i, x, 0:8]], 0)
                return jnp.concatenate([cells[i, x, 8:16], after(i)], 0)

            values = [pop(i) for i in range(19)]
            density, velocity = moments_of(values)
            for axis in range(3):
                at = AT_VEL + (axis * CX + x) * VEL
                if half == 0:
                    outer = jnp.where(row < VEL, low[at : at + 8], velocity[axis][0:8])
                    known = jnp.concatenate([outer, velocity[axis][8:16]], 0)
                else:
                    outer = jnp.where(row >= FULL, high[at - FULL : at - FULL + 8], velocity[axis][8:16])
                    known = jnp.concatenate([velocity[axis][0:8], outer], 0)
                at = axis * XY + x * EXT + half * 16
                vcat[at : at + 16, 0:NZ], vcat[at : at + 16, NZ:] = split(known)

            def put(i, value):
                base[i, x, rows] = value

            relaxed(values, density, velocity, is_fluid[rows] > 0.5, put)


def dense(cells, first, weights):
    offset = cells - first
    value = jnp.where(offset == 3.0, weights[3], 0.0)
    for k in (2, 1, 0):
        value = jnp.where(offset == float(k), weights[k], value)
    return value


def kernel_weights(frac):
    root = jnp.sqrt(1.0 + 4.0 * frac - 4.0 * frac * frac)
    second = (3.0 - 2.0 * frac + root) / 8.0
    third = (1.0 + 2.0 * frac + root) / 8.0
    return [0.5 - third, second, third, 0.5 - second]


def weights_kernel(markers, zcat, ys, state, work):
    left = lax.broadcasted_iota(jnp.int32, (6, LANES), 1) < 64
    for tile in range(16):
        one, two = markers[2 * tile], markers[2 * tile + 1]
        even = jnp.where(left, one, pltpu.roll(two, 64, 1))
        odd = jnp.where(left, pltpu.roll(one, 64, 1), two)
        kept = (even[3:4], odd[3:4], even[4:5], odd[2:3], odd[4:5], even[5:6], odd[5:6], even[0:1])
        for r, value in enumerate(kept):
            state[r, tile : tile + 1] = value
        for r, value in enumerate((odd[0:1], even[1:2], odd[1:2], even[2:3])):
            work[r, tile : tile + 1] = value
    for r, target, at in ((1, state, KX), (2, work, KY), (3, work, KZ)):
        for k, value in enumerate(kernel_weights(work[r])):
            target[at + k] = value

    z_cell = lax.broadcasted_iota(jnp.int32, (NZ, LANES), 0).astype(F32)
    y_cell = lax.broadcasted_iota(jnp.int32, (EXT, LANES), 0).astype(F32) - HALO
    for tile in range(16):
        cols = slice(tile * LANES, (tile + 1) * LANES)

        def row(r):
            return work[r, tile : tile + 1]

        zcat[0:NZ, cols], zcat[NZ : 2 * NZ, cols] = split(dense(z_cell, row(0), [row(KZ + k) for k in range(4)]))
        ys[:, cols] = dense(y_cell, state[7, tile : tile + 1], [row(KY + k) for k in range(4)])


def first_kernel(vcat, base, fluid, zcat, ys, given, up, down, push, state, work, weighted, spread):
    state[0:FORCE] = given[...]
    velocity = jnp.concatenate([vcat[...], vcat[:, 0:NZ]], 1)
    for pair in range(8):
        found = interpolated(velocity, zcat, slice(pair * 256, (pair + 1) * 256))
        for half in range(2):
            tile = 2 * pair + half
            for axis in range(3):
                work[axis, tile : tile + 1] = averaged(
                    found[axis * XY : (axis + 1) * XY, half * LANES : (half + 1) * LANES],
                    ys[:, tile * LANES : (tile + 1) * LANES],
                    [state[KX + x, tile : tile + 1] for x in range(CX)],
                )
    for axis in range(3):
        mean, disp = work[axis], state[4 + axis]
        state[FORCE + axis] = KAPPA * (state[axis] - mean) - state[3] * disp
        state[4 + axis] = disp + mean

    weigh(weighted, ys, lambda axis, tile: state[FORCE + axis, tile : tile + 1], state, OUTSIDE, EXT)
    spread[...] = contract(weighted[...], zcat[...])
    for p, x in enumerate(OUTSIDE):
        for tile in range(4):
            rows = slice(tile * 8, tile * 8 + 8)
            for axis, value in enumerate(spread_at(spread, p, tile, EXT, fluid[x, rows])):
                push[axis, p, rows] = value
    for p, faces, target in ((1, UP, up), (0, DOWN, down)):
        for j, index in enumerate(faces):
            force = along(index, [push[axis, p] for axis in range(3)])
            plane = base[index, OUTSIDE[p]] + (3.0 * WEIGHTS[index]) * force
            target[j] = moved(plane, index, TRIM)[0:INNER]


def inner_kernel(base, fluid, fluid_inner, push, ys, zcat, state, edge, found, inside, post, moving, velocities, weighted, spread):
    weigh(weighted, ys, lambda axis, tile: state[FORCE + axis, tile : tile + 1], state, INSIDE, EXT)
    spread[...] = contract(weighted[...], zcat[...])
    for x in range(CX):
        for tile in range(4):
            rows = slice(tile * 8, tile * 8 + 8)

            def put(i, value):
                post[i, x, rows] = value

            if x in INSIDE:
                force = spread_at(spread, x - 1, tile, EXT, fluid[x, rows])
            else:
                force = [push[axis, x // 3, rows] for axis in range(3)]
            forced(lambda i: base[i, x, rows], force, put)
    for index in range(19):
        for x in range(CX):
            source = x - DIRS[index][0]
            if not 0 <= source < CX:
                continue
            plane = moved(post[index, source], index, TRIM)[0:INNER]
            if x in INSIDE:
                moving[index, x - 1] = plane
            else:
                edge[index, x // 3] = plane
    for p, x in enumerate(INSIDE):
        for tile in range(3):
            rows = slice(tile * 8, tile * 8 + 8)
            values = [moving[i, p, rows] for i in range(19)]
            density, velocity = moments_of(values)
            for axis in range(3):
                at = (axis * 2 + p) * INNER + tile * 8
                velocities[at : at + 8] = velocity[axis]

            def put(i, value):
                inside[i, p, rows] = value

            relaxed(values, density, velocity, fluid_inner[x, rows] > 0.5, put)
    partial_means(velocities, zcat, ys, state, INSIDE, lambda axis, tile, value: found.__setitem__((axis, slice(tile, tile + 1)), value))


def partial_means(velocities, zcat, ys, state, planes, put):
    velocity = tripled(velocities[...])
    for pair in range(8):
        found = interpolated(velocity, zcat, slice(pair * 256, (pair + 1) * 256))
        for half in range(2):
            tile = 2 * pair + half
            y_rows = ys[TRIM : TRIM + INNER, tile * LANES : (tile + 1) * LANES]
            for axis in range(3):
                at = axis * 2 * INNER
                part = averaged(
                    found[at : at + 2 * INNER, half * LANES : (half + 1) * LANES],
                    y_rows,
                    [state[KX + x, tile : tile + 1] for x in planes],
                )
                put(axis, tile, part)


def edge_values(edge, up, down, x, rows):
    def value(i):
        if x == 0 and DIRS[i][0] == 1:
            return up[UP.index(i), rows]
        if x == CX - 1 and DIRS[i][0] == -1:
            return down[DOWN.index(i), rows]
        return edge[i, x // 3, rows]

    return [value(i) for i in range(19)]


def second_kernel(edge, up, down, ys, zcat, state, found, force, density, velocities, back, mean, rest):
    for p, x in enumerate(OUTSIDE):
        for tile in range(3):
            rows = slice(tile * 8, tile * 8 + 8)
            dense_at, velocity = moments_of(edge_values(edge, up, down, x, rows))
            density[p, rows] = dense_at
            for axis in range(3):
                at = (axis * 2 + p) * INNER + tile * 8
                velocities[at : at + 8] = velocity[axis]
    partial_means(velocities, zcat, ys, state, OUTSIDE, lambda axis, tile, value: mean.__setitem__((axis, slice(tile, tile + 1)), value))
    mine = (state[7] >= 0.0) & (state[7] < float(ROWS))
    moved_to, pulls = [], []
    for axis in range(3):
        average = found[axis] + mean[axis]
        disp = state[4 + axis]
        pull = KAPPA * (state[axis] - average) - state[3] * disp
        force[axis] = pull
        moved_to.append(jnp.where(mine, disp + average, 0.0))
        pulls.append(jnp.where(mine, pull, 0.0))
    values = moved_to + pulls
    left = lax.broadcasted_iota(jnp.int32, (16, LANES), 1) < 64
    for r in range(3):
        even, odd = values[2 * r], values[2 * r + 1]
        rest[0, r] = jnp.where(left, even, pltpu.roll(odd, 64, 1))
        rest[1, r] = jnp.where(left, pltpu.roll(even, 64, 1), odd)
        for tile in range(16):
            back[2 * tile, r : r + 1] = rest[0, r, tile : tile + 1]
            back[2 * tile + 1, r : r + 1] = rest[1, r, tile : tile + 1]


def third_kernel(
    edge, up, down, fluid, density, velocities, force, ys, zcat, state, out_up, out_down, post, weighted, spread, trimmed
):
    trimmed[...] = ys[TRIM : TRIM + INNER]
    weigh(weighted, trimmed, lambda axis, tile: force[axis, tile : tile + 1], state, OUTSIDE, INNER)
    spread[...] = contract(weighted[...], zcat[...])
    for p, x in enumerate(OUTSIDE):
        for tile in range(3):
            rows = slice(tile * 8, tile * 8 + 8)

            def put(i, value):
                post[i, p, rows] = value

            values = edge_values(edge, up, down, x, rows)
            velocity = [velocities[pl.ds((axis * 2 + p) * INNER + tile * 8, 8)] for axis in range(3)]
            is_fluid = fluid[x, rows]
            relaxed(values, density[p, rows], velocity, is_fluid > 0.5, put)
            pushed = spread_at(spread, p, tile, INNER, is_fluid)
            forced(lambda i: post[i, p, rows], pushed, put)
    for j, index in enumerate(UP):
        out_up[j] = moved(post[index, 1], index, HALO - TRIM)[0:ROWS]
    for j, index in enumerate(DOWN):
        out_down[j] = moved(post[index, 0], index, HALO - TRIM)[0:ROWS]


def stream_kernel(inside, outside, fluid, force, ys, zcat, state, out, post, weighted, spread, trimmed):
    trimmed[...] = ys[TRIM : TRIM + INNER]
    weigh(weighted, trimmed, lambda axis, tile: force[axis, tile : tile + 1], state, INSIDE, INNER)
    spread[...] = contract(weighted[...], zcat[...])
    for p, x in enumerate(INSIDE):
        for tile in range(3):
            rows = slice(tile * 8, tile * 8 + 8)

            def put(i, value):
                post[i, p, rows] = value

            forced(lambda i: inside[i, p, rows], spread_at(spread, p, tile, INNER, fluid[x, rows]), put)
    for index in range(19):
        for x in range(CX):
            source = x - DIRS[index][0]
            if 0 <= source < CX:
                plane = post[index, source - 1] if source in INSIDE else outside[index, source // 3]
                out[index, x] = moved(plane, index, HALO - TRIM)[0:ROWS]
            else:
                out[index, x] = jnp.zeros((ROWS, NZ), F32)


def fill_kernel(part, up, down, out, sems):
    copies = []
    for j, index in enumerate(UP):
        copies.append(pltpu.make_async_copy(up.at[j], out.at[index, 0], sems.at[j]))
    for j, index in enumerate(DOWN):
        copies.append(pltpu.make_async_copy(down.at[j], out.at[index, CX - 1], sems.at[5 + j]))
    for copy in copies:
        copy.start()
    for copy in copies:
        copy.wait()


IN_VMEM = pl.BlockSpec(memory_space=pltpu.VMEM)
ANYWHERE = pl.BlockSpec(memory_space=pl.ANY)


def near(x):
    return pltpu.with_memory_space_constraint(x, pltpu.VMEM)


def run(kernel, args, outs, scratch=(), cost=4_000_000):
    return pl.pallas_call(
        kernel,
        out_shape=outs,
        in_specs=[IN_VMEM] * len(args),
        out_specs=jax.tree.map(lambda _: IN_VMEM, outs, is_leaf=lambda leaf: not isinstance(leaf, tuple)),
        scratch_shapes=list(scratch),
        compiler_params=pltpu.CompilerParams(vmem_limit_bytes=24 * 2**20),
        cost_estimate=pl.CostEstimate(flops=0, transcendentals=0, bytes_accessed=cost),
    )(*args)


def ring(axis):
    peers = lax.axis_size(axis)
    forward = [(i, (i + 1) % peers) for i in range(peers)]
    return forward, [(j, i) for i, j in forward]


def parts(populations, solid, marker_corner, marker_frac, marker_target, stiffness, displacement):
    peers = lax.axis_size("sub")
    sub_up, sub_down = ring("sub")
    plate_up, plate_down = ring("plate")
    args = (populations, solid, marker_corner, marker_frac, marker_target, stiffness.reshape(1, 64), displacement)
    shape = (SENT_ROWS, NZ)
    sent, cells, bottom, top = pl.pallas_call(
        pack_kernel,
        out_shape=(
            jax.ShapeDtypeStruct((peers, 6, LANES), F32),
            pltpu.VMEM((20, CX, ROWS, NZ), F32),
            pltpu.VMEM(shape, F32),
            pltpu.VMEM(shape, F32),
        ),
        in_specs=[pl.BlockSpec(memory_space=pltpu.HBM)] * 7,
        out_specs=[IN_VMEM] * 4,
        scratch_shapes=[
            pltpu.VMEM((8, LANES), F32),
            pltpu.VMEM(solid.shape, jnp.int32),
            *[pltpu.VMEM(arg.shape, arg.dtype) for arg in args[2:]],
            pltpu.SemaphoreType.DMA((7,)),
        ],
        compiler_params=pltpu.CompilerParams(vmem_limit_bytes=8 * 2**20),
        name="pack_kernel",
    )(*[pltpu.with_memory_space_constraint(arg, pltpu.HBM) for arg in args])
    markers = lax.all_to_all(sent, "sub", 0, 0, tiled=True)
    low = lax.ppermute(bottom, "sub", sub_up)
    high = lax.ppermute(top, "sub", sub_down)
    zcat, ys, given = run(
        weights_kernel,
        (near(markers),),
        (
            pltpu.VMEM((2 * NZ, MARKERS), BF16),
            pltpu.VMEM((EXT, MARKERS), F32),
            pltpu.VMEM((FORCE, 16, LANES), F32),
        ),
        (pltpu.VMEM((WORK, 16, LANES), F32),),
    )
    vcat, base, fluid, fluid_inner = run(
        relax_kernel,
        (near(low), near(cells), near(high)),
        (
            pltpu.VMEM((3 * XY, 2 * NZ), BF16),
            pltpu.VMEM((19, CX, EXT, NZ), F32),
            pltpu.VMEM((CX, EXT, NZ), F32),
            pltpu.VMEM((CX, INNER, NZ), F32),
        ),
    )
    faces = (pltpu.VMEM((5, INNER, NZ), F32),) * 2
    plane_pairs = pltpu.VMEM((19, 2, INNER, NZ), F32)
    rows = pltpu.VMEM((3, 16, LANES), F32)

    def spreading(cells):
        return (pltpu.VMEM((12 * cells, MARKERS), BF16), pltpu.VMEM((12 * cells, 2 * NZ), F32))

    up, down, push, state = run(
        first_kernel,
        (near(vcat), near(base), near(fluid), near(zcat), near(ys), near(given)),
        (*faces, pltpu.VMEM((3, 2, EXT, NZ), F32), pltpu.VMEM((STATE, 16, LANES), F32)),
        (rows, *spreading(EXT)),
    )
    up = lax.ppermute(up, "plate", plate_up)
    down = lax.ppermute(down, "plate", plate_down)
    known = (near(ys), near(zcat), near(state))
    edge, found, inside = run(
        inner_kernel,
        (near(base), near(fluid), near(fluid_inner), near(push), *known),
        (plane_pairs, rows, pltpu.HBM((19, 2, INNER, NZ), F32)),
        (
            pltpu.VMEM((19, CX, EXT, NZ), F32),
            plane_pairs,
            pltpu.VMEM((6 * INNER, NZ), F32),
            *spreading(EXT),
        ),
        cost=12_000_000,
    )
    edges = (near(edge), near(up), near(down))
    force, density, velocities, back = run(
        second_kernel,
        (*edges, *known, near(found)),
        (
            rows,
            pltpu.VMEM((2, INNER, NZ), F32),
            pltpu.VMEM((6 * INNER, NZ), F32),
            jax.ShapeDtypeStruct((peers, 3, LANES), F32),
        ),
        (rows, pltpu.VMEM((2, 3, 16, LANES), F32)),
    )
    back = lax.all_to_all(back, "sub", 0, 0, tiled=True)
    trimmed = pltpu.VMEM((INNER, MARKERS), F32)
    up, down, outside = run(
        third_kernel,
        (*edges, near(fluid_inner), near(density), near(velocities), near(force), *known),
        (*[pltpu.VMEM((5, ROWS, NZ), F32)] * 2, plane_pairs),
        (*spreading(INNER), trimmed),
    )
    up = lax.ppermute(up, "plate", plate_up)
    down = lax.ppermute(down, "plate", plate_down)
    part = run(
        stream_kernel,
        (pltpu.with_memory_space_constraint(inside, pltpu.HBM), near(outside), near(fluid_inner), near(force), *known),
        jax.ShapeDtypeStruct((19, CX, ROWS, NZ), F32),
        (plane_pairs, *spreading(INNER), trimmed),
        cost=12_000_000,
    )
    out = pl.pallas_call(
        fill_kernel,
        out_shape=jax.ShapeDtypeStruct((19, CX, ROWS, NZ), F32),
        in_specs=[ANYWHERE, IN_VMEM, IN_VMEM],
        out_specs=ANYWHERE,
        scratch_shapes=[pltpu.SemaphoreType.DMA((10,))],
        input_output_aliases={0: 0},
        compiler_params=pltpu.CompilerParams(vmem_limit_bytes=8 * 2**20),
        name="fill_kernel",
    )(part, near(up), near(down))
    result = jnp.sum(back, 0).reshape(6, 64)
    return (out, result[:3], result[3:])


def solution(mesh):
    in_specs = (
        P(None, "plate", "sub", None),
        P("plate", "sub", None),
        P(None, ("plate", "sub")),
        P(None, ("plate", "sub")),
        P(None, ("plate", "sub")),
        P(("plate", "sub")),
        P(None, ("plate", "sub")),
    )
    out_specs = (
        P(None, "plate", "sub", None),
        P(None, ("plate", "sub")),
        P(None, ("plate", "sub")),
    )
    return jax.shard_map(parts, mesh=mesh, in_specs=in_specs, out_specs=out_specs, check_vma=False)
```

time: 54.9 us -> 54.6 us (level)
  blocking collectives: 0 us -> 18.1 us
  waiting for transfers between devices: 18.6 us -> 4.43 us
  starting transfers between devices: 24.1 us -> 17.7 us
  Pallas kernels: 9.76 us -> 11.9 us
    all_to_all x0 -> x1, blocking collectives: none -> 18.1 us  [parts(): markers = lax.all_to_all(sent, 'sub', 0, 0, tiled=True)]
    all_to_all x1 -> x0, waiting for transfers between devices: 11.4 us -> none  [parts(): markers = lax.all_to_all(sent, 'sub', 0, 0, tiled=True)]
    all_to_all x1 -> x0, starting transfers between devices: 6.43 us -> none  [parts(): markers = lax.all_to_all(sent, 'sub', 0, 0, tiled=True)]
    pallas_call x6 -> x7, Pallas kernels: 7.15 us -> 9.85 us  [run(): pl.pallas_call(kernel, out_shape=outs, in_specs=[IN_VMEM] * len(args), ou...]
    ppermute x2, waiting for transfers between devices: 2.82 us -> 0.19 us  [parts(): up = lax.ppermute(up, 'plate', plate_up)]
  transfers between devices with their start and end apart: 8 -> 7, of which waited for: 6 -> 4; matrix products, arithmetic and copies ran while one was open for 0% -> 0% of each run, Pallas kernels for 7% -> 13%
where the time goes in v2:
time: 54.6 us; the launch traced here: 53.6 us
  blocking collectives  18.1 us (33%)
  starting transfers between devices  17.7 us (32%)
  Pallas kernels  11.9 us (22%)
  waiting for transfers between devices  4.43 us (8%)
  between operations  0.71 us (1%)
  local copies, waits for them, and re-layouts  0.67 us (1%)
    all_to_all x1, blocking collectives, parts(): markers = lax.all_to_all(sent, 'sub', 0, 0, tiled=True)  18.1 us
    pallas_call x7, Pallas kernels, run(): pl.pallas_call(kernel, out_shape=outs, in_specs=[IN_VMEM] * len(args), ou...  9.85 us
    ppermute x1, starting transfers between devices, parts(): high = lax.ppermute(top, 'sub', sub_down)  7.83 us
    all_to_all x1, starting transfers between devices, parts(): back = lax.all_to_all(back, 'sub', 0, 0, tiled=True)  3.83 us
    ppermute x2, starting transfers between devices, parts(): down = lax.ppermute(down, 'plate', plate_down)  2.99 us
    ppermute x2, starting transfers between devices, parts(): up = lax.ppermute(up, 'plate', plate_up)  2.95 us
    all_to_all x1, waiting for transfers between devices, parts(): back = lax.all_to_all(back, 'sub', 0, 0, tiled=True)  2.63 us
    ppermute x2, waiting for transfers between devices, parts(): down = lax.ppermute(down, 'plate', plate_down)  1.61 us
  transfers between devices with their start and end apart: 7, of which 4 were waited for; matrix products, arithmetic and copies ran while one was open for 0% of the time, Pallas kernels for 13%

profile of v2, /device:TPU:8, one launch (start us, length us, event | category | flops | bytes accessed | tf_op | source)
XLA Modules:
  0.0 53.6 jit_solution(2701450408211708540)
XLA Ops:
  0.6 1.3 %pack_kernel.1 = (f32[32,6,128]{2,1,0:T(8,128)S(1)}, f32[20,4,16,128]{3,2,1,0:T(8,128)S(1)}, f32[456,128]{1,0:T(8,128)S(1)}, f32[456,128]{1,0:T(8,128)S(1)}) custom-call(f32[19,4,16,128]{3,2,1,0:T(8,128)} %own.1, s32[4,16,128]{2,1,0:T(8,128)} %solid.1, s32[3,64]{1,0:T(4,128)} %corner.1, f32[3,64]{1,0:T(4,128)} %frac.1, f32[3,64]{1,0:T(4,128)} %target.1, ...), custom_call_target="tpu_custom_call" | custom-call | tf_op jit(solution)/shard_map/pack_kernel/pallas_call | solution.py:529
  2.0 0.1 collective-permute-start
  2.1 7.8 %collective-permute-start.1 = (f32[456,128]{1,0:T(8,128)S(1)}, f32[456,128]{1,0:T(8,128)S(1)}, u32[]{:S(2)}, u32[]{:S(2)}) collective-permute-start(f32[456,128]{1,0:T(8,128)S(1)} %get-tuple-element.30), channel_id=1, source_target_pairs={{1,0},{2,1},{3,2},{4,3},{5,4},{6,5},{7,6},{8,7},{9,8},{10,9},{11,1... | collective-permute-start | bytes 700424 | tf_op jit(solution)/shard_map/ppermute | solution.py:550
  9.9 18.1 %all_to_all.10.markers = f32[32,6,128]{2,1,0:T(8,128)S(1)} all-to-all(f32[32,6,128]{2,1,0:T(8,128)S(1)} %get-tuple-element.35), channel_id=1, replica_groups=mesh['plate'=8,'sub'=32] {'sub'}, dimensions={0} | all-to-all | bytes 196608 | tf_op jit(solution)/shard_map/all_to_all | solution.py:548
  28.1 0.8 %shard_map.95 = (bf16[256,2048]{1,0:T(8,128)(2,1)S(1)}, f32[32,2048]{1,0:T(8,128)S(1)}, f32[12,16,128]{2,1,0:T(8,128)S(1)}) custom-call(f32[32,6,128]{2,1,0:T(8,128)S(1)} %all_to_all.10.markers), custom_call_target="tpu_custom_call" | custom-call | bytes 4000000 | tf_op jit(solution)/shard_map/pallas_call | solution.py:506
  28.8 0.0 collective-permute-done.low
  28.8 0.0 collective-permute-done.1.high
  28.9 0.6 %shard_map.94 = (bf16[384,256]{1,0:T(8,128)(2,1)S(1)}, f32[19,4,32,128]{3,2,1,0:T(8,128)S(1)}, f32[4,32,128]{2,1,0:T(8,128)S(1)}, f32[4,24,128]{2,1,0:T(8,128)S(1)}) custom-call(f32[456,128]{1,0:T(8,128)S(1)} %collective-permute-done.low, f32[20,4,16,128]{3,2,1,0:T(8,128)S(1)} %get-tuple-element.29.cells, f32[456,128]{1,0:T(8,128)S(1)} %collective-permute-done.1.high), custom_call_target="tpu_custom_call" | custom-call | bytes 4000000 | tf_op jit(solution)/shard_map/pallas_call | solution.py:506
  29.4 1.9 %shard_map.96 = (f32[5,24,128]{2,1,0:T(8,128)S(1)}, f32[5,24,128]{2,1,0:T(8,128)S(1)}, f32[3,2,32,128]{3,2,1,0:T(8,128)S(1)}, f32[15,16,128]{2,1,0:T(8,128)S(1)}) custom-call(bf16[384,256]{1,0:T(8,128)(2,1)S(1)} %get-tuple-element.34.vcat, f32[19,4,32,128]{3,2,1,0:T(8,128)S(1)} %get-tuple-element.31.base, f32[4,32,128]{2,1,0:T(8,128)S(1)} %get-tuple-element.32.fluid, ...), custom_call_target="tpu_custom_call" | custom-call | bytes 4000000 | tf_op jit(solution)/shard_map/pallas_call | solution.py:506
  31.3 0.7 %collective-permute-start.2 = (f32[5,24,128]{2,1,0:T(8,128)S(1)}, f32[5,24,128]{2,1,0:T(8,128)S(1)}, u32[]{:S(2)}, u32[]{:S(2)}) collective-permute-start(f32[5,24,128]{2,1,0:T(8,128)S(1)} %get-tuple-element.43), channel_id=1, source_target_pairs={{0,32},{32,64},{64,96},{96,128},{128,160},{160,192},{192,224},{224... | collective-permute-start | bytes 184328 | tf_op jit(solution)/shard_map/ppermute | solution.py:584
  32.0 2.3 %collective-permute-start.3 = (f32[5,24,128]{2,1,0:T(8,128)S(1)}, f32[5,24,128]{2,1,0:T(8,128)S(1)}, u32[]{:S(2)}, u32[]{:S(2)}) collective-permute-start(f32[5,24,128]{2,1,0:T(8,128)S(1)} %get-tuple-element.44), channel_id=1, source_target_pairs={{32,0},{64,32},{96,64},{128,96},{160,128},{192,160},{224,192},{0,2... | collective-permute-start | bytes 184328 | tf_op jit(solution)/shard_map/ppermute | solution.py:585
  34.3 2.0 %shard_map.97 = (f32[19,2,24,128]{3,2,1,0:T(8,128)S(1)}, f32[3,16,128]{2,1,0:T(8,128)S(1)}, f32[19,2,24,128]{3,2,1,0:T(8,128)}) custom-call(f32[19,4,32,128]{3,2,1,0:T(8,128)S(1)} %get-tuple-element.31.base, f32[4,32,128]{2,1,0:T(8,128)S(1)} %get-tuple-element.32.fluid, f32[4,24,128]{2,1,0:T(8,128)S(1)} %get-tuple-element.33.fluid_inner.fluid, ...), custom_call_target="tpu_custom_call" | custom-call | bytes 12000000 | tf_op jit(solution)/shard_map/pallas_call | solution.py:506
  36.3 0.2 collective-permute-done.2.up
  36.5 0.8 %collective-permute-done.3.down = f32[5,24,128]{2,1,0:T(8,128)S(1)} collective-permute-done((f32[5,24,128]{2,1,0:T(8,128)S(1)}, f32[5,24,128]{2,1,0:T(8,128)S(1)}, u32[]{:S(2)}, u32[]{:S(2)}) %collective-permute-start.3) | collective-permute-done | bytes 61472 | tf_op jit(solution)/shard_map/ppermute | solution.py:585
  37.3 1.2 %shard_map.98 = (f32[3,16,128]{2,1,0:T(8,128)S(1)}, f32[2,24,128]{2,1,0:T(8,128)S(1)}, f32[144,128]{1,0:T(8,128)S(1)}, f32[32,3,128]{2,1,0:T(4,128)}) custom-call(f32[19,2,24,128]{3,2,1,0:T(8,128)S(1)} %get-tuple-element.42.edge, f32[5,24,128]{2,1,0:T(8,128)S(1)} %collective-permute-done.2.up, f32[5,24,128]{2,1,0:T(8,128)S(1)} %collective-permute-done.3.down, ...), custom_call_target="tpu_custom_call" | custom-call | bytes 4000000 | tf_op jit(solution)/shard_map/pallas_call | solution.py:506
  38.5 3.8 %all-to-all-start.1 = ((f32[32,3,128]{2,1,0:T(4,128)}), f32[32,3,128]{2,1,0:T(4,128)S(1)}, u32[]{:S(2)}, u32[]{:S(2)}) async-start(f32[32,3,128]{2,1,0:T(4,128)} %get-tuple-element.52), calls=%async_computation.1 | async-start | bytes 131072 | tf_op jit(solution)/shard_map/all_to_all | solution.py:611
  42.4 0.8 %shard_map.99 = (f32[5,16,128]{2,1,0:T(8,128)S(1)}, f32[5,16,128]{2,1,0:T(8,128)S(1)}, f32[19,2,24,128]{3,2,1,0:T(8,128)S(1)}) custom-call(f32[19,2,24,128]{3,2,1,0:T(8,128)S(1)} %get-tuple-element.42.edge, f32[5,24,128]{2,1,0:T(8,128)S(1)} %collective-permute-done.2.up, f32[5,24,128]{2,1,0:T(8,128)S(1)} %collective-permute-done.3.down, ...), custom_call_target="tpu_custom_call" | custom-call | bytes 4000000 | tf_op jit(solution)/shard_map/pallas_call | solution.py:506
  43.2 2.3 %collective-permute-start.4 = (f32[5,16,128]{2,1,0:T(8,128)S(1)}, f32[5,16,128]{2,1,0:T(8,128)S(1)}, u32[]{:S(2)}, u32[]{:S(2)}) collective-permute-start(f32[5,16,128]{2,1,0:T(8,128)S(1)} %get-tuple-element.50), channel_id=1, source_target_pairs={{0,32},{32,64},{64,96},{96,128},{128,160},{160,192},{192,224},{224... | collective-permute-start | bytes 122888 | tf_op jit(solution)/shard_map/ppermute | solution.py:619
  45.4 0.7 %collective-permute-start.5 = (f32[5,16,128]{2,1,0:T(8,128)S(1)}, f32[5,16,128]{2,1,0:T(8,128)S(1)}, u32[]{:S(2)}, u32[]{:S(2)}) collective-permute-start(f32[5,16,128]{2,1,0:T(8,128)S(1)} %get-tuple-element.51), channel_id=1, source_target_pairs={{32,0},{64,32},{96,64},{128,96},{160,128},{192,160},{224,192},{0,2... | collective-permute-start | bytes 122888 | tf_op jit(solution)/shard_map/ppermute | solution.py:620
  46.1 2.6 %shard_map.100.part = f32[19,4,16,128]{3,2,1,0:T(8,128)} custom-call(f32[19,2,24,128]{3,2,1,0:T(8,128)} %get-tuple-element.41.inside, f32[19,2,24,128]{3,2,1,0:T(8,128)S(1)} %get-tuple-element.49.outside, f32[4,24,128]{2,1,0:T(8,128)S(1)} %get-tuple-element.33.fluid_inner.fluid, f32[3,16,128]{2,1,0:T(8,128)S(1)} %get-tuple-element.48.force, ...), custom_call_target="tpu_custom_call" | custom-call | bytes 12000000 | tf_op jit(solution)/shard_map/pallas_call | solution.py:506
  48.7 0.0 collective-permute-done.4.up
  48.7 0.8 %collective-permute-done.5.down = f32[5,16,128]{2,1,0:T(8,128)S(1)} collective-permute-done((f32[5,16,128]{2,1,0:T(8,128)S(1)}, f32[5,16,128]{2,1,0:T(8,128)S(1)}, u32[]{:S(2)}, u32[]{:S(2)}) %collective-permute-start.5) | collective-permute-done | bytes 40992 | tf_op jit(solution)/shard_map/ppermute | solution.py:620
  49.5 0.7 %fill_kernel.1 = f32[19,4,16,128]{3,2,1,0:T(8,128)} custom-call(f32[19,4,16,128]{3,2,1,0:T(8,128)} %shard_map.100.part, f32[5,16,128]{2,1,0:T(8,128)S(1)} %collective-permute-done.4.up, f32[5,16,128]{2,1,0:T(8,128)S(1)} %collective-permute-done.5.down), custom_call_target="tpu_custom_call", output_to_operand_aliasing={{}: (0, {})} | custom-call | tf_op jit(solution)/shard_map/fill_kernel/pallas_call | solution.py:628
  50.3 2.6 %all-to-all-done.1 = f32[32,3,128]{2,1,0:T(4,128)S(1)} async-done(((f32[32,3,128]{2,1,0:T(4,128)}), f32[32,3,128]{2,1,0:T(4,128)S(1)}, u32[]{:S(2)}, u32[]{:S(2)}) %all-to-all-start.1) | async-done | bytes 49184 | tf_op jit(solution)/shard_map/all_to_all | solution.py:611
  52.9 0.1 reshape.13
  53.0 0.6 %fusion = (f32[3,64]{1,0:T(4,128)}, f32[3,64]{1,0:T(4,128)}) fusion(f32[6,64]{1,0:T(8,128)S(1)} %reshape.13), kind=kLoop, calls=%fused_computation | loop fusion | bytes 3072 | tf_op jit(solution)/shard_map/slice | solution.py:639
  (1 shorter events, 0.0 us)
Async XLA Ops:
  2.0 26.8 %collective-permute-start = (f32[456,128]{1,0:T(8,128)S(1)}, f32[456,128]{1,0:T(8,128)S(1)}, u32[]{:S(2)}, u32[]{:S(2)}) collective-permute-start(f32[456,128]{1,0:T(8,128)S(1)} %get-tuple-element.28), channel_id=1, source_target_pairs={{0,1},{1,2},{2,3},{3,4},{4,5},{5,6},{6,7},{7,8},{8,9},{9,10},{10,1... | collective-permute-start | bytes 700424 | tf_op jit(solution)/shard_map/ppermute | solution.py:549
  2.1 26.8 %collective-permute-start.1 = (f32[456,128]{1,0:T(8,128)S(1)}, f32[456,128]{1,0:T(8,128)S(1)}, u32[]{:S(2)}, u32[]{:S(2)}) collective-permute-start(f32[456,128]{1,0:T(8,128)S(1)} %get-tuple-element.30), channel_id=1, source_target_pairs={{1,0},{2,1},{3,2},{4,3},{5,4},{6,5},{7,6},{8,7},{9,8},{10,9},{11,1... | collective-permute-start | bytes 700424 | tf_op jit(solution)/shard_map/ppermute | solution.py:550
  31.3 5.2 %collective-permute-start.2 = (f32[5,24,128]{2,1,0:T(8,128)S(1)}, f32[5,24,128]{2,1,0:T(8,128)S(1)}, u32[]{:S(2)}, u32[]{:S(2)}) collective-permute-start(f32[5,24,128]{2,1,0:T(8,128)S(1)} %get-tuple-element.43), channel_id=1, source_target_pairs={{0,32},{32,64},{64,96},{96,128},{128,160},{160,192},{192,224},{224... | collective-permute-start | bytes 184328 | tf_op jit(solution)/shard_map/ppermute | solution.py:584
  32.0 5.3 %collective-permute-start.3 = (f32[5,24,128]{2,1,0:T(8,128)S(1)}, f32[5,24,128]{2,1,0:T(8,128)S(1)}, u32[]{:S(2)}, u32[]{:S(2)}) collective-permute-start(f32[5,24,128]{2,1,0:T(8,128)S(1)} %get-tuple-element.44), channel_id=1, source_target_pairs={{32,0},{64,32},{96,64},{128,96},{160,128},{192,160},{224,192},{0,2... | collective-permute-start | bytes 184328 | tf_op jit(solution)/shard_map/ppermute | solution.py:585
  38.5 14.4 %all-to-all-start.1 = ((f32[32,3,128]{2,1,0:T(4,128)}), f32[32,3,128]{2,1,0:T(4,128)S(1)}, u32[]{:S(2)}, u32[]{:S(2)}) async-start(f32[32,3,128]{2,1,0:T(4,128)} %get-tuple-element.52), calls=%async_computation.1 | async-start | bytes 131072 | tf_op jit(solution)/shard_map/all_to_all | solution.py:611
  43.2 5.5 %collective-permute-start.4 = (f32[5,16,128]{2,1,0:T(8,128)S(1)}, f32[5,16,128]{2,1,0:T(8,128)S(1)}, u32[]{:S(2)}, u32[]{:S(2)}) collective-permute-start(f32[5,16,128]{2,1,0:T(8,128)S(1)} %get-tuple-element.50), channel_id=1, source_target_pairs={{0,32},{32,64},{64,96},{96,128},{128,160},{160,192},{192,224},{224... | collective-permute-start | bytes 122888 | tf_op jit(solution)/shard_map/ppermute | solution.py:619
  45.4 4.1 %collective-permute-start.5 = (f32[5,16,128]{2,1,0:T(8,128)S(1)}, f32[5,16,128]{2,1,0:T(8,128)S(1)}, u32[]{:S(2)}, u32[]{:S(2)}) collective-permute-start(f32[5,16,128]{2,1,0:T(8,128)S(1)} %get-tuple-element.51), channel_id=1, source_target_pairs={{32,0},{64,32},{96,64},{128,96},{160,128},{192,160},{224,192},{0,2... | collective-permute-start | bytes 122888 | tf_op jit(solution)/shard_map/ppermute | solution.py:620

commit v3 on v2

--- a/solution.py
+++ b/solution.py
@@ -38,7 +38,6 @@
 HALO = 8
 EXT = ROWS + 2 * HALO
 NZ = 128
-XY = CX * EXT
 TRIM = 4
 INNER = EXT - 2 * TRIM
 MARKERS = 2048
@@ -172,7 +171,7 @@
     return block
 
 
-def pack_kernel(own, solid, corner, frac, target, stiffness, disp, sent, cells, bottom, top, block, walls, *held):
+def pack_kernel(own, solid, corner, frac, target, stiffness, disp, sent, cells, bottom, top, block, walls, blocks, *held):
     sems = held[-1]
     held = held[:-1]
     small = [
@@ -201,7 +200,9 @@
     for peer in range(peers):
         away = whole - float(peer * ROWS)
         away = away - jnp.where(away >= period / 2, period, jnp.where(away < -period / 2, -period, 0.0))
-        sent[peer] = jnp.where(first, away, whole)
+        blocks[peer] = jnp.where(first, away, whole)
+    going = pltpu.make_async_copy(blocks, sent, sems.at[7])
+    going.start()
     for copy in large:
         copy.wait()
     for buffer in (bottom, top):
@@ -217,49 +218,50 @@
             for axis, value in enumerate(moments_of(values[0:19])[1]):
                 at = AT_VEL + (axis * CX + x) * VEL
                 buffer[at : at + VEL] = value[vel : vel + VEL]
-
-
-def relax_kernel(low, cells, high, vcat, base, fluid, fluid_inner):
-    row = lax.broadcasted_iota(jnp.int32, (8, NZ), 0)
+    going.wait()
+
+
+def own_kernel(cells, vcat, base, walls):
     for x in range(CX):
-
-        def before(i):
-            at = AT_PLANE + (i * CX + x) * FULL - VEL
-            return low[at : at + 8]
-
-        def after(i):
+        walls[x] = cells[19, x]
+        values = [cells[i, x] for i in range(19)]
+        density, velocity = moments_of(values)
+        for axis in range(3):
+            at = (axis * CX + x) * ROWS
+            vcat[at : at + ROWS, 0:NZ], vcat[at : at + ROWS, NZ:] = split(velocity[axis])
+
+        def put(i, value):
+            base[i, x] = value
+
+        relaxed(values, density, velocity, cells[19, x] < 0.5, put)
+
+
+def outer_kernel(low, walls, high, vcat, base, fluid, fluid_inner):
+    row = lax.broadcasted_iota(jnp.int32, (16, NZ), 0)
+    received = (row < VEL) | (row >= HALO + FULL)
+    for x in range(CX):
+
+        def pop(i):
             at = AT_PLANE + (i * CX + x) * FULL
-            return high[at : at + 8]
-
-        wall = jnp.concatenate([before(19), cells[19, x], after(19)], 0)
-        is_fluid = 1.0 - wall
+            return jnp.concatenate([low[at - VEL : at - VEL + 8], high[at : at + 8]], 0)
+
+        wall = pop(19)
+        is_fluid = 1.0 - jnp.concatenate([wall[0:8], walls[x], wall[8:16]], 0)
         fluid[x] = is_fluid
         fluid_inner[x] = pltpu.roll(is_fluid, EXT - TRIM, 0)[0:INNER]
-        for half in range(2):
-            rows = slice(half * 16, half * 16 + 16)
-
-            def pop(i):
-                if half == 0:
-                    return jnp.concatenate([before(i), cells[i, x, 0:8]], 0)
-                return jnp.concatenate([cells[i, x, 8:16], after(i)], 0)
-
-            values = [pop(i) for i in range(19)]
-            density, velocity = moments_of(values)
-            for axis in range(3):
-                at = AT_VEL + (axis * CX + x) * VEL
-                if half == 0:
-                    outer = jnp.where(row < VEL, low[at : at + 8], velocity[axis][0:8])
-                    known = jnp.concatenate([outer, velocity[axis][8:16]], 0)
-                else:
-                    outer = jnp.where(row >= FULL, high[at - FULL : at - FULL + 8], velocity[axis][8:16])
-                    known = jnp.concatenate([velocity[axis][0:8], outer], 0)
-                at = axis * XY + x * EXT + half * 16
-                vcat[at : at + 16, 0:NZ], vcat[at : at + 16, NZ:] = split(known)
-
-            def put(i, value):
-                base[i, x, rows] = value
-
-            relaxed(values, density, velocity, is_fluid[rows] > 0.5, put)
+        values = [pop(i) for i in range(19)]
+        density, velocity = moments_of(values)
+        for axis in range(3):
+            at = AT_VEL + (axis * CX + x) * VEL
+            sent = jnp.concatenate([low[at : at + 8], high[at - FULL : at - FULL + 8]], 0)
+            known = jnp.where(received, sent, velocity[axis])
+            at = (axis * CX + x) * ROWS
+            vcat[at : at + ROWS, 0:NZ], vcat[at : at + ROWS, NZ:] = split(known)
+
+        def put(i, value):
+            base[i, x] = value
+
+        relaxed(values, density, velocity, wall < 0.5, put)
 
 
 def dense(cells, first, weights):
@@ -304,19 +306,24 @@
         ys[:, cols] = dense(y_cell, state[7, tile : tile + 1], [row(KY + k) for k in range(4)])
 
 
-def first_kernel(vcat, base, fluid, zcat, ys, given, up, down, push, state, work, weighted, spread):
+def first_kernel(
+    vown, vouter, own, outer, fluid, zcat, ys, given, up, down, push, state, work, weighted, spread
+):
     state[0:FORCE] = given[...]
-    velocity = jnp.concatenate([vcat[...], vcat[:, 0:NZ]], 1)
+    velocity = jnp.concatenate([vown[...], vouter[...]], 0)
+    velocity = jnp.concatenate([velocity, velocity[:, 0:NZ]], 1)
     for pair in range(8):
         found = interpolated(velocity, zcat, slice(pair * 256, (pair + 1) * 256))
         for half in range(2):
             tile = 2 * pair + half
             for axis in range(3):
-                work[axis, tile : tile + 1] = averaged(
-                    found[axis * XY : (axis + 1) * XY, half * LANES : (half + 1) * LANES],
-                    ys[:, tile * LANES : (tile + 1) * LANES],
-                    [state[KX + x, tile : tile + 1] for x in range(CX)],
-                )
+                at, lanes = axis * CX * ROWS, slice(half * LANES, (half + 1) * LANES)
+                cols = slice(tile * LANES, (tile + 1) * LANES)
+                kx = [state[KX + x, tile : tile + 1] for x in range(CX)]
+                inner = averaged(found[at : at + CX * ROWS, lanes], ys[HALO : HALO + ROWS, cols], kx)
+                y_outer = jnp.concatenate([ys[0:HALO, cols], ys[HALO + ROWS :, cols]], 0)
+                at += 3 * CX * ROWS
+                work[axis, tile : tile + 1] = inner + averaged(found[at : at + CX * ROWS, lanes], y_outer, kx)
     for axis in range(3):
         mean, disp = work[axis], state[4 + axis]
         state[FORCE + axis] = KAPPA * (state[axis] - mean) - state[3] * disp
@@ -332,11 +339,16 @@
     for p, faces, target in ((1, UP, up), (0, DOWN, down)):
         for j, index in enumerate(faces):
             force = along(index, [push[axis, p] for axis in range(3)])
-            plane = base[index, OUTSIDE[p]] + (3.0 * WEIGHTS[index]) * force
+            x = OUTSIDE[p]
+            plane = jnp.concatenate([outer[index, x, 0:HALO], own[index, x], outer[index, x, HALO:]], 0)
+            plane = plane + (3.0 * WEIGHTS[index]) * force
             target[j] = moved(plane, index, TRIM)[0:INNER]
 
 
-def inner_kernel(base, fluid, fluid_inner, push, ys, zcat, state, edge, found, inside, post, moving, velocities, weighted, spread):
+def inner_kernel(
+    own, outer, fluid, fluid_inner, push, ys, zcat, state, edge, found, inside, trimmed, post, moving, velocities, weighted, spread
+):
+    trimmed[...] = ys[TRIM : TRIM + INNER]
     weigh(weighted, ys, lambda axis, tile: state[FORCE + axis, tile : tile + 1], state, INSIDE, EXT)
     spread[...] = contract(weighted[...], zcat[...])
     for x in range(CX):
@@ -350,7 +362,13 @@
                 force = spread_at(spread, x - 1, tile, EXT, fluid[x, rows])
             else:
                 force = [push[axis, x // 3, rows] for axis in range(3)]
-            forced(lambda i: base[i, x, rows], force, put)
+
+            def base(i):
+                if tile in (0, 3):
+                    return outer[i, x, 0:8] if tile == 0 else outer[i, x, 8:16]
+                return own[i, x, tile * 8 - 8 : tile * 8]
+
+            forced(base, force, put)
     for index in range(19):
         for x in range(CX):
             source = x - DIRS[index][0]
@@ -374,7 +392,7 @@
                 inside[i, p, rows] = value
 
             relaxed(values, density, velocity, fluid_inner[x, rows] > 0.5, put)
-    partial_means(velocities, zcat, ys, state, INSIDE, lambda axis, tile, value: found.__setitem__((axis, slice(tile, tile + 1)), value))
+    partial_means(velocities, zcat, trimmed, state, INSIDE, lambda axis, tile, value: found.__setitem__((axis, slice(tile, tile + 1)), value))
 
 
 def partial_means(velocities, zcat, ys, state, planes, put):
@@ -383,7 +401,7 @@
         found = interpolated(velocity, zcat, slice(pair * 256, (pair + 1) * 256))
         for half in range(2):
             tile = 2 * pair + half
-            y_rows = ys[TRIM : TRIM + INNER, tile * LANES : (tile + 1) * LANES]
+            y_rows = ys[:, tile * LANES : (tile + 1) * LANES]
             for axis in range(3):
                 at = axis * 2 * INNER
                 part = averaged(
@@ -436,10 +454,9 @@
 
 
 def third_kernel(
-    edge, up, down, fluid, density, velocities, force, ys, zcat, state, out_up, out_down, post, weighted, spread, trimmed
+    edge, up, down, fluid, density, velocities, force, ys, zcat, state, out_up, out_down, post, weighted, spread
 ):
-    trimmed[...] = ys[TRIM : TRIM + INNER]
-    weigh(weighted, trimmed, lambda axis, tile: force[axis, tile : tile + 1], state, OUTSIDE, INNER)
+    weigh(weighted, ys, lambda axis, tile: force[axis, tile : tile + 1], state, OUTSIDE, INNER)
     spread[...] = contract(weighted[...], zcat[...])
     for p, x in enumerate(OUTSIDE):
         for tile in range(3):
@@ -460,9 +477,8 @@
         out_down[j] = moved(post[index, 0], index, HALO - TRIM)[0:ROWS]
 
 
-def stream_kernel(inside, outside, fluid, force, ys, zcat, state, out, post, weighted, spread, trimmed):
-    trimmed[...] = ys[TRIM : TRIM + INNER]
-    weigh(weighted, trimmed, lambda axis, tile: force[axis, tile : tile + 1], state, INSIDE, INNER)
+def stream_kernel(inside, outside, fluid, force, ys, zcat, state, out, post, weighted, spread):
+    weigh(weighted, ys, lambda axis, tile: force[axis, tile : tile + 1], state, INSIDE, INNER)
     spread[...] = contract(weighted[...], zcat[...])
     for p, x in enumerate(INSIDE):
         for tile in range(3):
@@ -535,12 +551,13 @@
             pltpu.VMEM(shape, F32),
         ),
         in_specs=[pl.BlockSpec(memory_space=pltpu.HBM)] * 7,
-        out_specs=[IN_VMEM] * 4,
+        out_specs=[pl.BlockSpec(memory_space=pltpu.HBM), *[IN_VMEM] * 3],
         scratch_shapes=[
             pltpu.VMEM((8, LANES), F32),
             pltpu.VMEM(solid.shape, jnp.int32),
+            pltpu.VMEM((peers, 6, LANES), F32),
             *[pltpu.VMEM(arg.shape, arg.dtype) for arg in args[2:]],
-            pltpu.SemaphoreType.DMA((7,)),
+            pltpu.SemaphoreType.DMA((8,)),
         ],
         compiler_params=pltpu.CompilerParams(vmem_limit_bytes=8 * 2**20),
         name="pack_kernel",
@@ -558,15 +575,12 @@
         ),
         (pltpu.VMEM((WORK, 16, LANES), F32),),
     )
-    vcat, base, fluid, fluid_inner = run(
-        relax_kernel,
-        (near(low), near(cells), near(high)),
-        (
-            pltpu.VMEM((3 * XY, 2 * NZ), BF16),
-            pltpu.VMEM((19, CX, EXT, NZ), F32),
-            pltpu.VMEM((CX, EXT, NZ), F32),
-            pltpu.VMEM((CX, INNER, NZ), F32),
-        ),
+    half = (pltpu.VMEM((3 * CX * ROWS, 2 * NZ), BF16), pltpu.VMEM((19, CX, ROWS, NZ), F32))
+    vown, own, walls = run(own_kernel, (near(cells),), (*half, pltpu.VMEM((CX, ROWS, NZ), F32)))
+    vouter, outer, fluid, fluid_inner = run(
+        outer_kernel,
+        (near(low), near(walls), near(high)),
+        (*half, pltpu.VMEM((CX, EXT, NZ), F32), pltpu.VMEM((CX, INNER, NZ), F32)),
     )
     faces = (pltpu.VMEM((5, INNER, NZ), F32),) * 2
     plane_pairs = pltpu.VMEM((19, 2, INNER, NZ), F32)
@@ -577,17 +591,18 @@
 
     up, down, push, state = run(
         first_kernel,
-        (near(vcat), near(base), near(fluid), near(zcat), near(ys), near(given)),
+        (near(vown), near(vouter), near(own), near(outer), near(fluid), near(zcat), near(ys), near(given)),
         (*faces, pltpu.VMEM((3, 2, EXT, NZ), F32), pltpu.VMEM((STATE, 16, LANES), F32)),
         (rows, *spreading(EXT)),
     )
     up = lax.ppermute(up, "plate", plate_up)
     down = lax.ppermute(down, "plate", plate_down)
     known = (near(ys), near(zcat), near(state))
-    edge, found, inside = run(
+    trimmed = pltpu.VMEM((INNER, MARKERS), F32)
+    edge, found, inside, ys = run(
         inner_kernel,
-        (near(base), near(fluid), near(fluid_inner), near(push), *known),
-        (plane_pairs, rows, pltpu.HBM((19, 2, INNER, NZ), F32)),
+        (near(own), near(outer), near(fluid), near(fluid_inner), near(push), *known),
+        (plane_pairs, rows, pltpu.HBM((19, 2, INNER, NZ), F32), trimmed),
         (
             pltpu.VMEM((19, CX, EXT, NZ), F32),
             plane_pairs,
@@ -596,6 +611,7 @@
         ),
         cost=12_000_000,
     )
+    known = (near(ys), near(zcat), near(state))
     edges = (near(edge), near(up), near(down))
     force, density, velocities, back = run(
         second_kernel,
@@ -609,12 +625,11 @@
         (rows, pltpu.VMEM((2, 3, 16, LANES), F32)),
     )
     back = lax.all_to_all(back, "sub", 0, 0, tiled=True)
-    trimmed = pltpu.VMEM((INNER, MARKERS), F32)
     up, down, outside = run(
         third_kernel,
         (*edges, near(fluid_inner), near(density), near(velocities), near(force), *known),
         (*[pltpu.VMEM((5, ROWS, NZ), F32)] * 2, plane_pairs),
-        (*spreading(INNER), trimmed),
+        spreading(INNER),
     )
     up = lax.ppermute(up, "plate", plate_up)
     down = lax.ppermute(down, "plate", plate_down)
@@ -622,7 +637,7 @@
         stream_kernel,
         (pltpu.with_memory_space_constraint(inside, pltpu.HBM), near(outside), near(fluid_inner), near(force), *known),
         jax.ShapeDtypeStruct((19, CX, ROWS, NZ), F32),
-        (plane_pairs, *spreading(INNER), trimmed),
+        (plane_pairs, *spreading(INNER)),
         cost=12_000_000,
     )
     out = pl.pallas_call(

time: 54.6 us -> 55.2 us (1.011)
  the two profiles are of different devices: /device:TPU:8 before, /device:TPU:1 now
where the time goes in v3:
time: 55.2 us; the launch traced here: 54.9 us
  starting transfers between devices  28.6 us (52%)
  Pallas kernels  12.7 us (23%)
  waiting for transfers between devices  12.2 us (22%)
  between operations  0.71 us (1%)
  local copies, waits for them, and re-layouts  0.67 us (1%)
    all_to_all x1, starting transfers between devices, parts(): markers = lax.all_to_all(sent, 'sub', 0, 0, tiled=True)  12.2 us
    pallas_call x8, Pallas kernels, run(): pl.pallas_call(kernel, out_shape=outs, in_specs=[IN_VMEM] * len(args), ou...  10.4 us
    all_to_all x1, waiting for transfers between devices, parts(): markers = lax.all_to_all(sent, 'sub', 0, 0, tiled=True)  10.2 us
    all_to_all x1, starting transfers between devices, parts(): back = lax.all_to_all(back, 'sub', 0, 0, tiled=True)  5.72 us
    ppermute x2, starting transfers between devices, parts(): down = lax.ppermute(down, 'plate', plate_down)  5.69 us
    ppermute x1, starting transfers between devices, parts(): low = lax.ppermute(bottom, 'sub', sub_up)  3.09 us
    all_to_all x1, waiting for transfers between devices, parts(): back = lax.all_to_all(back, 'sub', 0, 0, tiled=True)  1.96 us
    pallas_call x1, Pallas kernels, parts(): pl.pallas_call(pack_kernel, out_shape=(jax.ShapeDtypeStruct((peers, 6, LA...  1.56 us
  transfers between devices with their start and end apart: 8, of which 2 were waited for; matrix products, arithmetic and copies ran while one was open for 0% of the time, Pallas kernels for 14%

profile of v3, /device:TPU:1, one launch (start us, length us, event | category | flops | bytes accessed | tf_op | source)
XLA Modules:
  0.0 54.9 jit_solution(12369731198090885668)
XLA Ops:
  0.6 1.6 %pack_kernel.1 = (f32[32,6,128]{2,1,0:T(8,128)}, f32[20,4,16,128]{3,2,1,0:T(8,128)S(1)}, f32[456,128]{1,0:T(8,128)S(1)}, f32[456,128]{1,0:T(8,128)S(1)}) custom-call(f32[19,4,16,128]{3,2,1,0:T(8,128)} %own.1, s32[4,16,128]{2,1,0:T(8,128)} %solid.1, s32[3,64]{1,0:T(4,128)} %corner.1, f32[3,64]{1,0:T(4,128)} %frac.1, f32[3,64]{1,0:T(4,128)} %target.1, ...), custom_call_target="tpu_custom_call" | custom-call | tf_op jit(solution)/shard_map/pack_kernel/pallas_call | solution.py:545
  2.2 3.1 %collective-permute-start = (f32[456,128]{1,0:T(8,128)S(1)}, f32[456,128]{1,0:T(8,128)S(1)}, u32[]{:S(2)}, u32[]{:S(2)}) collective-permute-start(f32[456,128]{1,0:T(8,128)S(1)} %get-tuple-element.34), channel_id=1, source_target_pairs={{0,1},{1,2},{2,3},{3,4},{4,5},{5,6},{6,7},{7,8},{8,9},{9,10},{10,1... | collective-permute-start | bytes 700424 | tf_op jit(solution)/shard_map/ppermute | solution.py:566
  5.3 0.3 collective-permute-start.1
  5.6 12.2 %all-to-all-start = ((f32[32,6,128]{2,1,0:T(8,128)}), f32[32,6,128]{2,1,0:T(8,128)S(1)}, u32[]{:S(2)}, u32[]{:S(2)}) async-start(f32[32,6,128]{2,1,0:T(8,128)} %get-tuple-element.42), calls=%async_computation | async-start | bytes 262144 | tf_op jit(solution)/shard_map/all_to_all | solution.py:565
  17.8 0.3 shard_map.94
  18.1 10.2 %all-to-all-done.markers = f32[32,6,128]{2,1,0:T(8,128)S(1)} async-done(((f32[32,6,128]{2,1,0:T(8,128)}), f32[32,6,128]{2,1,0:T(8,128)S(1)}, u32[]{:S(2)}, u32[]{:S(2)}) %all-to-all-start) | async-done | bytes 98336 | tf_op jit(solution)/shard_map/all_to_all | solution.py:565
  28.3 0.8 %shard_map.96 = (bf16[256,2048]{1,0:T(8,128)(2,1)S(1)}, f32[32,2048]{1,0:T(8,128)S(1)}, f32[12,16,128]{2,1,0:T(8,128)S(1)}) custom-call(f32[32,6,128]{2,1,0:T(8,128)S(1)} %all-to-all-done.markers), custom_call_target="tpu_custom_call" | custom-call | bytes 4000000 | tf_op jit(solution)/shard_map/pallas_call | solution.py:522
  29.1 0.0 collective-permute-done.low
  29.1 0.0 collective-permute-done.1.high
  29.1 0.3 shard_map.95
  29.4 1.9 %shard_map.97 = (f32[5,24,128]{2,1,0:T(8,128)S(1)}, f32[5,24,128]{2,1,0:T(8,128)S(1)}, f32[3,2,32,128]{3,2,1,0:T(8,128)S(1)}, f32[15,16,128]{2,1,0:T(8,128)S(1)}) custom-call(bf16[192,256]{1,0:T(8,128)(2,1)S(1)} %get-tuple-element.40.vown, bf16[192,256]{1,0:T(8,128)(2,1)S(1)} %get-tuple-element.41.vouter, f32[19,4,16,128]{3,2,1,0:T(8,128)S(1)} %get-tuple-element.33.own, ...), custom_call_target="tpu_custom_call" | custom-call | bytes 4000000 | tf_op jit(solution)/shard_map/pallas_call | solution.py:522
  31.3 0.4 collective-permute-start.2
  31.7 3.3 %collective-permute-start.3 = (f32[5,24,128]{2,1,0:T(8,128)S(1)}, f32[5,24,128]{2,1,0:T(8,128)S(1)}, u32[]{:S(2)}, u32[]{:S(2)}) collective-permute-start(f32[5,24,128]{2,1,0:T(8,128)S(1)} %get-tuple-element.51), channel_id=1, source_target_pairs={{32,0},{64,32},{96,64},{128,96},{160,128},{192,160},{224,192},{0,2... | collective-permute-start | bytes 184328 | tf_op jit(solution)/shard_map/ppermute | solution.py:599
  35.0 2.6 %shard_map.98 = (f32[19,2,24,128]{3,2,1,0:T(8,128)S(1)}, f32[3,16,128]{2,1,0:T(8,128)S(1)}, f32[19,2,24,128]{3,2,1,0:T(8,128)}, f32[24,2048]{1,0:T(8,128)S(1)}) custom-call(f32[19,4,16,128]{3,2,1,0:T(8,128)S(1)} %get-tuple-element.33.own, f32[19,4,16,128]{3,2,1,0:T(8,128)S(1)} %get-tuple-element.37.outer, f32[4,32,128]{2,1,0:T(8,128)S(1)} %get-tuple-element.38.fluid, ...), custom_call_target="tpu_custom_call" | custom-call | bytes 12000000 | tf_op jit(solution)/shard_map/pallas_call | solution.py:522
  37.5 0.0 collective-permute-done.2.up
  37.5 0.0 collective-permute-done.3.down
  37.6 1.2 %shard_map.99 = (f32[3,16,128]{2,1,0:T(8,128)S(1)}, f32[2,24,128]{2,1,0:T(8,128)S(1)}, f32[144,128]{1,0:T(8,128)S(1)}, f32[32,3,128]{2,1,0:T(4,128)}) custom-call(f32[19,2,24,128]{3,2,1,0:T(8,128)S(1)} %get-tuple-element.49.edge, f32[5,24,128]{2,1,0:T(8,128)S(1)} %collective-permute-done.2.up, f32[5,24,128]{2,1,0:T(8,128)S(1)} %collective-permute-done.3.down, ...), custom_call_target="tpu_custom_call" | custom-call | bytes 4000000 | tf_op jit(solution)/shard_map/pallas_call | solution.py:522
  38.8 5.7 %all-to-all-start.1 = ((f32[32,3,128]{2,1,0:T(4,128)}), f32[32,3,128]{2,1,0:T(4,128)S(1)}, u32[]{:S(2)}, u32[]{:S(2)}) async-start(f32[32,3,128]{2,1,0:T(4,128)} %get-tuple-element.60), calls=%async_computation.1 | async-start | bytes 131072 | tf_op jit(solution)/shard_map/all_to_all | solution.py:627
  44.5 0.8 %shard_map.100 = (f32[5,16,128]{2,1,0:T(8,128)S(1)}, f32[5,16,128]{2,1,0:T(8,128)S(1)}, f32[19,2,24,128]{3,2,1,0:T(8,128)S(1)}) custom-call(f32[19,2,24,128]{3,2,1,0:T(8,128)S(1)} %get-tuple-element.49.edge, f32[5,24,128]{2,1,0:T(8,128)S(1)} %collective-permute-done.2.up, f32[5,24,128]{2,1,0:T(8,128)S(1)} %collective-permute-done.3.down, ...), custom_call_target="tpu_custom_call" | custom-call | bytes 4000000 | tf_op jit(solution)/shard_map/pallas_call | solution.py:522
  45.3 1.2 %collective-permute-start.4 = (f32[5,16,128]{2,1,0:T(8,128)S(1)}, f32[5,16,128]{2,1,0:T(8,128)S(1)}, u32[]{:S(2)}, u32[]{:S(2)}) collective-permute-start(f32[5,16,128]{2,1,0:T(8,128)S(1)} %get-tuple-element.58), channel_id=1, source_target_pairs={{0,32},{32,64},{64,96},{96,128},{128,160},{160,192},{192,224},{224... | collective-permute-start | bytes 122888 | tf_op jit(solution)/shard_map/ppermute | solution.py:634
  46.5 2.4 %collective-permute-start.5 = (f32[5,16,128]{2,1,0:T(8,128)S(1)}, f32[5,16,128]{2,1,0:T(8,128)S(1)}, u32[]{:S(2)}, u32[]{:S(2)}) collective-permute-start(f32[5,16,128]{2,1,0:T(8,128)S(1)} %get-tuple-element.59), channel_id=1, source_target_pairs={{32,0},{64,32},{96,64},{128,96},{160,128},{192,160},{224,192},{0,2... | collective-permute-start | bytes 122888 | tf_op jit(solution)/shard_map/ppermute | solution.py:635
  48.9 2.6 %shard_map.101.part = f32[19,4,16,128]{3,2,1,0:T(8,128)} custom-call(f32[19,2,24,128]{3,2,1,0:T(8,128)} %get-tuple-element.48.inside, f32[19,2,24,128]{3,2,1,0:T(8,128)S(1)} %get-tuple-element.57.outside, f32[4,24,128]{2,1,0:T(8,128)S(1)} %get-tuple-element.39.fluid_inner.fluid, f32[3,16,128]{2,1,0:T(8,128)S(1)} %get-tuple-element.56.force, ...), custom_call_target="tpu_custom_call" | custom-call | bytes 12000000 | tf_op jit(solution)/shard_map/pallas_call | solution.py:522
  51.5 0.0 collective-permute-done.4.up
  51.5 0.0 collective-permute-done.5.down
  51.5 0.7 %fill_kernel.1 = f32[19,4,16,128]{3,2,1,0:T(8,128)} custom-call(f32[19,4,16,128]{3,2,1,0:T(8,128)} %shard_map.101.part, f32[5,16,128]{2,1,0:T(8,128)S(1)} %collective-permute-done.4.up, f32[5,16,128]{2,1,0:T(8,128)S(1)} %collective-permute-done.5.down), custom_call_target="tpu_custom_call", output_to_operand_aliasing={{}: (0, {})} | custom-call | tf_op jit(solution)/shard_map/fill_kernel/pallas_call | solution.py:643
  52.2 2.0 %all-to-all-done.1 = f32[32,3,128]{2,1,0:T(4,128)S(1)} async-done(((f32[32,3,128]{2,1,0:T(4,128)}), f32[32,3,128]{2,1,0:T(4,128)S(1)}, u32[]{:S(2)}, u32[]{:S(2)}) %all-to-all-start.1) | async-done | bytes 49184 | tf_op jit(solution)/shard_map/all_to_all | solution.py:627
  54.2 0.1 reshape.13
  54.3 0.6 %fusion = (f32[3,64]{1,0:T(4,128)}, f32[3,64]{1,0:T(4,128)}) fusion(f32[6,64]{1,0:T(8,128)S(1)} %reshape.13), kind=kLoop, calls=%fused_computation | loop fusion | bytes 3072 | tf_op jit(solution)/shard_map/slice | solution.py:654
  (1 shorter events, 0.0 us)
Async XLA Ops:
  2.2 26.9 %collective-permute-start = (f32[456,128]{1,0:T(8,128)S(1)}, f32[456,128]{1,0:T(8,128)S(1)}, u32[]{:S(2)}, u32[]{:S(2)}) collective-permute-start(f32[456,128]{1,0:T(8,128)S(1)} %get-tuple-element.34), channel_id=1, source_target_pairs={{0,1},{1,2},{2,3},{3,4},{4,5},{5,6},{6,7},{7,8},{8,9},{9,10},{10,1... | collective-permute-start | bytes 700424 | tf_op jit(solution)/shard_map/ppermute | solution.py:566
  5.3 23.8 %collective-permute-start.1 = (f32[456,128]{1,0:T(8,128)S(1)}, f32[456,128]{1,0:T(8,128)S(1)}, u32[]{:S(2)}, u32[]{:S(2)}) collective-permute-start(f32[456,128]{1,0:T(8,128)S(1)} %get-tuple-element.36), channel_id=1, source_target_pairs={{1,0},{2,1},{3,2},{4,3},{5,4},{6,5},{7,6},{8,7},{9,8},{10,9},{11,1... | collective-permute-start | bytes 700424 | tf_op jit(solution)/shard_map/ppermute | solution.py:567
  5.6 22.7 %all-to-all-start = ((f32[32,6,128]{2,1,0:T(8,128)}), f32[32,6,128]{2,1,0:T(8,128)S(1)}, u32[]{:S(2)}, u32[]{:S(2)}) async-start(f32[32,6,128]{2,1,0:T(8,128)} %get-tuple-element.42), calls=%async_computation | async-start | bytes 262144 | tf_op jit(solution)/shard_map/all_to_all | solution.py:565
  31.3 6.2 %collective-permute-start.2 = (f32[5,24,128]{2,1,0:T(8,128)S(1)}, f32[5,24,128]{2,1,0:T(8,128)S(1)}, u32[]{:S(2)}, u32[]{:S(2)}) collective-permute-start(f32[5,24,128]{2,1,0:T(8,128)S(1)} %get-tuple-element.50), channel_id=1, source_target_pairs={{0,32},{32,64},{64,96},{96,128},{128,160},{160,192},{192,224},{224... | collective-permute-start | bytes 184328 | tf_op jit(solution)/shard_map/ppermute | solution.py:598
  31.7 5.9 %collective-permute-start.3 = (f32[5,24,128]{2,1,0:T(8,128)S(1)}, f32[5,24,128]{2,1,0:T(8,128)S(1)}, u32[]{:S(2)}, u32[]{:S(2)}) collective-permute-start(f32[5,24,128]{2,1,0:T(8,128)S(1)} %get-tuple-element.51), channel_id=1, source_target_pairs={{32,0},{64,32},{96,64},{128,96},{160,128},{192,160},{224,192},{0,2... | collective-permute-start | bytes 184328 | tf_op jit(solution)/shard_map/ppermute | solution.py:599
  38.8 15.4 %all-to-all-start.1 = ((f32[32,3,128]{2,1,0:T(4,128)}), f32[32,3,128]{2,1,0:T(4,128)S(1)}, u32[]{:S(2)}, u32[]{:S(2)}) async-start(f32[32,3,128]{2,1,0:T(4,128)} %get-tuple-element.60), calls=%async_computation.1 | async-start | bytes 131072 | tf_op jit(solution)/shard_map/all_to_all | solution.py:627
  45.3 6.2 %collective-permute-start.4 = (f32[5,16,128]{2,1,0:T(8,128)S(1)}, f32[5,16,128]{2,1,0:T(8,128)S(1)}, u32[]{:S(2)}, u32[]{:S(2)}) collective-permute-start(f32[5,16,128]{2,1,0:T(8,128)S(1)} %get-tuple-element.58), channel_id=1, source_target_pairs={{0,32},{32,64},{64,96},{96,128},{128,160},{160,192},{192,224},{224... | collective-permute-start | bytes 122888 | tf_op jit(solution)/shard_map/ppermute | solution.py:634
  46.5 5.0 %collective-permute-start.5 = (f32[5,16,128]{2,1,0:T(8,128)S(1)}, f32[5,16,128]{2,1,0:T(8,128)S(1)}, u32[]{:S(2)}, u32[]{:S(2)}) collective-permute-start(f32[5,16,128]{2,1,0:T(8,128)S(1)} %get-tuple-element.59), channel_id=1, source_target_pairs={{32,0},{64,32},{96,64},{128,96},{160,128},{192,160},{224,192},{0,2... | collective-permute-start | bytes 122888 | tf_op jit(solution)/shard_map/ppermute | solution.py:635

commit v4 on v3

--- a/solution.py
+++ b/solution.py
@@ -200,7 +200,9 @@
     for peer in range(peers):
         away = whole - float(peer * ROWS)
         away = away - jnp.where(away >= period / 2, period, jnp.where(away < -period / 2, -period, 0.0))
-        blocks[peer] = jnp.where(first, away, whole)
+        adjusted = jnp.where(first, away, whole)
+        for pair in range(3):
+            blocks[peer, pair] = adjusted[2 * pair : 2 * pair + 2]
     going = pltpu.make_async_copy(blocks, sent, sems.at[7])
     going.start()
     for copy in large:
@@ -280,15 +282,19 @@
 
 
 def weights_kernel(markers, zcat, ys, state, work):
-    left = lax.broadcasted_iota(jnp.int32, (6, LANES), 1) < 64
+    left = lax.broadcasted_iota(jnp.int32, (2, LANES), 1) < 64
     for tile in range(16):
-        one, two = markers[2 * tile], markers[2 * tile + 1]
-        even = jnp.where(left, one, pltpu.roll(two, 64, 1))
-        odd = jnp.where(left, pltpu.roll(one, 64, 1), two)
-        kept = (even[3:4], odd[3:4], even[4:5], odd[2:3], odd[4:5], even[5:6], odd[5:6], even[0:1])
+        even, odd = [], []
+        for pair in range(3):
+            one, two = markers[2 * tile, pair], markers[2 * tile + 1, pair]
+            evens = jnp.where(left, one, pltpu.roll(two, 64, 1))
+            odds = jnp.where(left, pltpu.roll(one, 64, 1), two)
+            even += [evens[0:1], evens[1:2]]
+            odd += [odds[0:1], odds[1:2]]
+        kept = (even[3], odd[3], even[4], odd[2], odd[4], even[5], odd[5], even[0])
         for r, value in enumerate(kept):
             state[r, tile : tile + 1] = value
-        for r, value in enumerate((odd[0:1], even[1:2], odd[1:2], even[2:3])):
+        for r, value in enumerate((odd[0], even[1], odd[1], even[2])):
             work[r, tile : tile + 1] = value
     for r, target, at in ((1, state, KX), (2, work, KY), (3, work, KZ)):
         for k, value in enumerate(kernel_weights(work[r])):
@@ -449,8 +455,8 @@
         rest[0, r] = jnp.where(left, even, pltpu.roll(odd, 64, 1))
         rest[1, r] = jnp.where(left, pltpu.roll(even, 64, 1), odd)
         for tile in range(16):
-            back[2 * tile, r : r + 1] = rest[0, r, tile : tile + 1]
-            back[2 * tile + 1, r : r + 1] = rest[1, r, tile : tile + 1]
+            back[2 * tile, r] = rest[0, r, tile : tile + 1]
+            back[2 * tile + 1, r] = rest[1, r, tile : tile + 1]
 
 
 def third_kernel(
@@ -545,7 +551,7 @@
     sent, cells, bottom, top = pl.pallas_call(
         pack_kernel,
         out_shape=(
-            jax.ShapeDtypeStruct((peers, 6, LANES), F32),
+            jax.ShapeDtypeStruct((peers, 3, 2, LANES), F32),
             pltpu.VMEM((20, CX, ROWS, NZ), F32),
             pltpu.VMEM(shape, F32),
             pltpu.VMEM(shape, F32),
@@ -555,7 +561,7 @@
         scratch_shapes=[
             pltpu.VMEM((8, LANES), F32),
             pltpu.VMEM(solid.shape, jnp.int32),
-            pltpu.VMEM((peers, 6, LANES), F32),
+            pltpu.VMEM((peers, 3, 2, LANES), F32),
             *[pltpu.VMEM(arg.shape, arg.dtype) for arg in args[2:]],
             pltpu.SemaphoreType.DMA((8,)),
         ],
@@ -620,7 +626,7 @@
             rows,
             pltpu.VMEM((2, INNER, NZ), F32),
             pltpu.VMEM((6 * INNER, NZ), F32),
-            jax.ShapeDtypeStruct((peers, 3, LANES), F32),
+            jax.ShapeDtypeStruct((peers, 3, 1, LANES), F32),
         ),
         (rows, pltpu.VMEM((2, 3, 16, LANES), F32)),
     )

time: 55.2 us -> 54.5 us (0.987)
  waiting for transfers between devices: 12.2 us -> 11.5 us
    all_to_all x1, waiting for transfers between devices: 10.2 us -> 9.6 us  [parts(): markers = lax.all_to_all(sent, 'sub', 0, 0, tiled=True)]
where the time goes in v4:
time: 54.5 us; the launch traced here: 54.3 us
  starting transfers between devices  28.5 us (52%)
  Pallas kernels  12.8 us (23%)
  waiting for transfers between devices  11.5 us (21%)
  between operations  0.71 us (1%)
  local copies, waits for them, and re-layouts  0.67 us (1%)
    all_to_all x1, starting transfers between devices, parts(): markers = lax.all_to_all(sent, 'sub', 0, 0, tiled=True)  12.2 us
    pallas_call x8, Pallas kernels, run(): pl.pallas_call(kernel, out_shape=outs, in_specs=[IN_VMEM] * len(args), ou...  10.5 us
    all_to_all x1, waiting for transfers between devices, parts(): markers = lax.all_to_all(sent, 'sub', 0, 0, tiled=True)  9.6 us
    ppermute x2, starting transfers between devices, parts(): down = lax.ppermute(down, 'plate', plate_down)  5.7 us
    all_to_all x1, starting transfers between devices, parts(): back = lax.all_to_all(back, 'sub', 0, 0, tiled=True)  5.67 us
    ppermute x1, starting transfers between devices, parts(): low = lax.ppermute(bottom, 'sub', sub_up)  3.09 us
    all_to_all x1, waiting for transfers between devices, parts(): back = lax.all_to_all(back, 'sub', 0, 0, tiled=True)  1.89 us
    pallas_call x1, Pallas kernels, parts(): pl.pallas_call(pack_kernel, out_shape=(jax.ShapeDtypeStruct((peers, 3, 2,...  1.56 us
  transfers between devices with their start and end apart: 8, of which 2 were waited for; matrix products, arithmetic and copies ran while one was open for 0% of the time, Pallas kernels for 14%

profile of v4, /device:TPU:1, one launch (start us, length us, event | category | flops | bytes accessed | tf_op | source)
XLA Modules:
  0.0 54.3 jit_solution(5438579452696694008)
XLA Ops:
  0.6 1.6 %pack_kernel.1 = (f32[32,3,2,128]{3,2,1,0:T(2,128)}, f32[20,4,16,128]{3,2,1,0:T(8,128)S(1)}, f32[456,128]{1,0:T(8,128)S(1)}, f32[456,128]{1,0:T(8,128)S(1)}) custom-call(f32[19,4,16,128]{3,2,1,0:T(8,128)} %own.1, s32[4,16,128]{2,1,0:T(8,128)} %solid.1, s32[3,64]{1,0:T(4,128)} %corner.1, f32[3,64]{1,0:T(4,128)} %frac.1, f32[3,64]{1,0:T(4,128)} %target.1, ...), custom_call_target="tpu_custom_call" | custom-call | tf_op jit(solution)/shard_map/pack_kernel/pallas_call | solution.py:551
  2.2 3.1 %collective-permute-start = (f32[456,128]{1,0:T(8,128)S(1)}, f32[456,128]{1,0:T(8,128)S(1)}, u32[]{:S(2)}, u32[]{:S(2)}) collective-permute-start(f32[456,128]{1,0:T(8,128)S(1)} %get-tuple-element.34), channel_id=1, source_target_pairs={{0,1},{1,2},{2,3},{3,4},{4,5},{5,6},{6,7},{7,8},{8,9},{9,10},{10,1... | collective-permute-start | bytes 700424 | tf_op jit(solution)/shard_map/ppermute | solution.py:572
  5.3 0.3 collective-permute-start.1
  5.6 12.2 %all-to-all-start = ((f32[32,3,2,128]{3,2,1,0:T(2,128)}), f32[32,3,2,128]{3,2,1,0:T(2,128)S(1)}, u32[]{:S(2)}, u32[]{:S(2)}) async-start(f32[32,3,2,128]{3,2,1,0:T(2,128)} %get-tuple-element.42), calls=%async_computation | async-start | bytes 196608 | tf_op jit(solution)/shard_map/all_to_all | solution.py:571
  17.8 0.3 shard_map.94
  18.1 9.6 %all-to-all-done.markers = f32[32,3,2,128]{3,2,1,0:T(2,128)S(1)} async-done(((f32[32,3,2,128]{3,2,1,0:T(2,128)}), f32[32,3,2,128]{3,2,1,0:T(2,128)S(1)}, u32[]{:S(2)}, u32[]{:S(2)}) %all-to-all-start) | async-done | bytes 98336 | tf_op jit(solution)/shard_map/all_to_all | solution.py:571
  27.7 0.9 %shard_map.96 = (bf16[256,2048]{1,0:T(8,128)(2,1)S(1)}, f32[32,2048]{1,0:T(8,128)S(1)}, f32[12,16,128]{2,1,0:T(8,128)S(1)}) custom-call(f32[32,3,2,128]{3,2,1,0:T(2,128)S(1)} %all-to-all-done.markers), custom_call_target="tpu_custom_call" | custom-call | bytes 4000000 | tf_op jit(solution)/shard_map/pallas_call | solution.py:528
  28.6 0.0 collective-permute-done.low
  28.6 0.0 collective-permute-done.1.high
  28.6 0.3 shard_map.95
  28.9 1.9 %shard_map.97 = (f32[5,24,128]{2,1,0:T(8,128)S(1)}, f32[5,24,128]{2,1,0:T(8,128)S(1)}, f32[3,2,32,128]{3,2,1,0:T(8,128)S(1)}, f32[15,16,128]{2,1,0:T(8,128)S(1)}) custom-call(bf16[192,256]{1,0:T(8,128)(2,1)S(1)} %get-tuple-element.40.vown, bf16[192,256]{1,0:T(8,128)(2,1)S(1)} %get-tuple-element.41.vouter, f32[19,4,16,128]{3,2,1,0:T(8,128)S(1)} %get-tuple-element.33.own, ...), custom_call_target="tpu_custom_call" | custom-call | bytes 4000000 | tf_op jit(solution)/shard_map/pallas_call | solution.py:528
  30.8 0.4 collective-permute-start.2
  31.2 3.3 %collective-permute-start.3 = (f32[5,24,128]{2,1,0:T(8,128)S(1)}, f32[5,24,128]{2,1,0:T(8,128)S(1)}, u32[]{:S(2)}, u32[]{:S(2)}) collective-permute-start(f32[5,24,128]{2,1,0:T(8,128)S(1)} %get-tuple-element.51), channel_id=1, source_target_pairs={{32,0},{64,32},{96,64},{128,96},{160,128},{192,160},{224,192},{0,2... | collective-permute-start | bytes 184328 | tf_op jit(solution)/shard_map/ppermute | solution.py:605
  34.4 2.6 %shard_map.98 = (f32[19,2,24,128]{3,2,1,0:T(8,128)S(1)}, f32[3,16,128]{2,1,0:T(8,128)S(1)}, f32[19,2,24,128]{3,2,1,0:T(8,128)}, f32[24,2048]{1,0:T(8,128)S(1)}) custom-call(f32[19,4,16,128]{3,2,1,0:T(8,128)S(1)} %get-tuple-element.33.own, f32[19,4,16,128]{3,2,1,0:T(8,128)S(1)} %get-tuple-element.37.outer, f32[4,32,128]{2,1,0:T(8,128)S(1)} %get-tuple-element.38.fluid, ...), custom_call_target="tpu_custom_call" | custom-call | bytes 12000000 | tf_op jit(solution)/shard_map/pallas_call | solution.py:528
  37.0 0.0 collective-permute-done.2.up
  37.0 0.0 collective-permute-done.3.down
  37.0 1.2 %shard_map.99 = (f32[3,16,128]{2,1,0:T(8,128)S(1)}, f32[2,24,128]{2,1,0:T(8,128)S(1)}, f32[144,128]{1,0:T(8,128)S(1)}, f32[32,3,1,128]{3,2,1,0:T(1,128)}) custom-call(f32[19,2,24,128]{3,2,1,0:T(8,128)S(1)} %get-tuple-element.49.edge, f32[5,24,128]{2,1,0:T(8,128)S(1)} %collective-permute-done.2.up, f32[5,24,128]{2,1,0:T(8,128)S(1)} %collective-permute-done.3.down, ...), custom_call_target="tpu_custom_call" | custom-call | bytes 4000000 | tf_op jit(solution)/shard_map/pallas_call | solution.py:528
  38.3 5.7 %all-to-all-start.1 = ((f32[32,3,1,128]{3,2,1,0:T(1,128)}), f32[32,3,1,128]{3,2,1,0:T(1,128)S(1)}, u32[]{:S(2)}, u32[]{:S(2)}) async-start(f32[32,3,1,128]{3,2,1,0:T(1,128)} %get-tuple-element.60), calls=%async_computation.1 | async-start | bytes 98304 | tf_op jit(solution)/shard_map/all_to_all | solution.py:633
  43.9 0.8 %shard_map.100 = (f32[5,16,128]{2,1,0:T(8,128)S(1)}, f32[5,16,128]{2,1,0:T(8,128)S(1)}, f32[19,2,24,128]{3,2,1,0:T(8,128)S(1)}) custom-call(f32[19,2,24,128]{3,2,1,0:T(8,128)S(1)} %get-tuple-element.49.edge, f32[5,24,128]{2,1,0:T(8,128)S(1)} %collective-permute-done.2.up, f32[5,24,128]{2,1,0:T(8,128)S(1)} %collective-permute-done.3.down, ...), custom_call_target="tpu_custom_call" | custom-call | bytes 4000000 | tf_op jit(solution)/shard_map/pallas_call | solution.py:528
  44.7 1.2 %collective-permute-start.4 = (f32[5,16,128]{2,1,0:T(8,128)S(1)}, f32[5,16,128]{2,1,0:T(8,128)S(1)}, u32[]{:S(2)}, u32[]{:S(2)}) collective-permute-start(f32[5,16,128]{2,1,0:T(8,128)S(1)} %get-tuple-element.58), channel_id=1, source_target_pairs={{0,32},{32,64},{64,96},{96,128},{128,160},{160,192},{192,224},{224... | collective-permute-start | bytes 122888 | tf_op jit(solution)/shard_map/ppermute | solution.py:640
  45.9 2.4 %collective-permute-start.5 = (f32[5,16,128]{2,1,0:T(8,128)S(1)}, f32[5,16,128]{2,1,0:T(8,128)S(1)}, u32[]{:S(2)}, u32[]{:S(2)}) collective-permute-start(f32[5,16,128]{2,1,0:T(8,128)S(1)} %get-tuple-element.59), channel_id=1, source_target_pairs={{32,0},{64,32},{96,64},{128,96},{160,128},{192,160},{224,192},{0,2... | collective-permute-start | bytes 122888 | tf_op jit(solution)/shard_map/ppermute | solution.py:641
  48.3 2.6 %shard_map.101.part = f32[19,4,16,128]{3,2,1,0:T(8,128)} custom-call(f32[19,2,24,128]{3,2,1,0:T(8,128)} %get-tuple-element.48.inside, f32[19,2,24,128]{3,2,1,0:T(8,128)S(1)} %get-tuple-element.57.outside, f32[4,24,128]{2,1,0:T(8,128)S(1)} %get-tuple-element.39.fluid_inner.fluid, f32[3,16,128]{2,1,0:T(8,128)S(1)} %get-tuple-element.56.force, ...), custom_call_target="tpu_custom_call" | custom-call | bytes 12000000 | tf_op jit(solution)/shard_map/pallas_call | solution.py:528
  50.9 0.0 collective-permute-done.4.up
  50.9 0.0 collective-permute-done.5.down
  50.9 0.7 %fill_kernel.1 = f32[19,4,16,128]{3,2,1,0:T(8,128)} custom-call(f32[19,4,16,128]{3,2,1,0:T(8,128)} %shard_map.101.part, f32[5,16,128]{2,1,0:T(8,128)S(1)} %collective-permute-done.4.up, f32[5,16,128]{2,1,0:T(8,128)S(1)} %collective-permute-done.5.down), custom_call_target="tpu_custom_call", output_to_operand_aliasing={{}: (0, {})} | custom-call | tf_op jit(solution)/shard_map/fill_kernel/pallas_call | solution.py:649
  51.6 1.9 %all-to-all-done.1 = f32[32,3,1,128]{3,2,1,0:T(1,128)S(1)} async-done(((f32[32,3,1,128]{3,2,1,0:T(1,128)}), f32[32,3,1,128]{3,2,1,0:T(1,128)S(1)}, u32[]{:S(2)}, u32[]{:S(2)}) %all-to-all-start.1) | async-done | bytes 49184 | tf_op jit(solution)/shard_map/all_to_all | solution.py:633
  53.5 0.1 reduce_sum.9
  53.6 0.1 reshape.15
  53.7 0.6 %fusion = (f32[3,64]{1,0:T(4,128)}, f32[3,64]{1,0:T(4,128)}) fusion(f32[6,64]{1,0:T(8,128)S(1)} %reshape.15), kind=kLoop, calls=%fused_computation | loop fusion | bytes 3072 | tf_op jit(solution)/shard_map/slice | solution.py:660
Async XLA Ops:
  2.2 26.4 %collective-permute-start = (f32[456,128]{1,0:T(8,128)S(1)}, f32[456,128]{1,0:T(8,128)S(1)}, u32[]{:S(2)}, u32[]{:S(2)}) collective-permute-start(f32[456,128]{1,0:T(8,128)S(1)} %get-tuple-element.34), channel_id=1, source_target_pairs={{0,1},{1,2},{2,3},{3,4},{4,5},{5,6},{6,7},{7,8},{8,9},{9,10},{10,1... | collective-permute-start | bytes 700424 | tf_op jit(solution)/shard_map/ppermute | solution.py:572
  5.3 23.3 %collective-permute-start.1 = (f32[456,128]{1,0:T(8,128)S(1)}, f32[456,128]{1,0:T(8,128)S(1)}, u32[]{:S(2)}, u32[]{:S(2)}) collective-permute-start(f32[456,128]{1,0:T(8,128)S(1)} %get-tuple-element.36), channel_id=1, source_target_pairs={{1,0},{2,1},{3,2},{4,3},{5,4},{6,5},{7,6},{8,7},{9,8},{10,9},{11,1... | collective-permute-start | bytes 700424 | tf_op jit(solution)/shard_map/ppermute | solution.py:573
  5.6 22.1 %all-to-all-start = ((f32[32,3,2,128]{3,2,1,0:T(2,128)}), f32[32,3,2,128]{3,2,1,0:T(2,128)S(1)}, u32[]{:S(2)}, u32[]{:S(2)}) async-start(f32[32,3,2,128]{3,2,1,0:T(2,128)} %get-tuple-element.42), calls=%async_computation | async-start | bytes 196608 | tf_op jit(solution)/shard_map/all_to_all | solution.py:571
  30.8 6.2 %collective-permute-start.2 = (f32[5,24,128]{2,1,0:T(8,128)S(1)}, f32[5,24,128]{2,1,0:T(8,128)S(1)}, u32[]{:S(2)}, u32[]{:S(2)}) collective-permute-start(f32[5,24,128]{2,1,0:T(8,128)S(1)} %get-tuple-element.50), channel_id=1, source_target_pairs={{0,32},{32,64},{64,96},{96,128},{128,160},{160,192},{192,224},{224... | collective-permute-start | bytes 184328 | tf_op jit(solution)/shard_map/ppermute | solution.py:604
  31.2 5.9 %collective-permute-start.3 = (f32[5,24,128]{2,1,0:T(8,128)S(1)}, f32[5,24,128]{2,1,0:T(8,128)S(1)}, u32[]{:S(2)}, u32[]{:S(2)}) collective-permute-start(f32[5,24,128]{2,1,0:T(8,128)S(1)} %get-tuple-element.51), channel_id=1, source_target_pairs={{32,0},{64,32},{96,64},{128,96},{160,128},{192,160},{224,192},{0,2... | collective-permute-start | bytes 184328 | tf_op jit(solution)/shard_map/ppermute | solution.py:605
  38.3 15.3 %all-to-all-start.1 = ((f32[32,3,1,128]{3,2,1,0:T(1,128)}), f32[32,3,1,128]{3,2,1,0:T(1,128)S(1)}, u32[]{:S(2)}, u32[]{:S(2)}) async-start(f32[32,3,1,128]{3,2,1,0:T(1,128)} %get-tuple-element.60), calls=%async_computation.1 | async-start | bytes 98304 | tf_op jit(solution)/shard_map/all_to_all | solution.py:633
  44.7 6.2 %collective-permute-start.4 = (f32[5,16,128]{2,1,0:T(8,128)S(1)}, f32[5,16,128]{2,1,0:T(8,128)S(1)}, u32[]{:S(2)}, u32[]{:S(2)}) collective-permute-start(f32[5,16,128]{2,1,0:T(8,128)S(1)} %get-tuple-element.58), channel_id=1, source_target_pairs={{0,32},{32,64},{64,96},{96,128},{128,160},{160,192},{192,224},{224... | collective-permute-start | bytes 122888 | tf_op jit(solution)/shard_map/ppermute | solution.py:640
  45.9 5.0 %collective-permute-start.5 = (f32[5,16,128]{2,1,0:T(8,128)S(1)}, f32[5,16,128]{2,1,0:T(8,128)S(1)}, u32[]{:S(2)}, u32[]{:S(2)}) collective-permute-start(f32[5,16,128]{2,1,0:T(8,128)S(1)} %get-tuple-element.59), channel_id=1, source_target_pairs={{32,0},{64,32},{96,64},{128,96},{160,128},{192,160},{224,192},{0,2... | collective-permute-start | bytes 122888 | tf_op jit(solution)/shard_map/ppermute | solution.py:641

commit v5 on v4

--- a/solution.py
+++ b/solution.py
@@ -514,6 +514,14 @@
         copy.start()
     for copy in copies:
         copy.wait()
+
+
+def tail_kernel(back, moved_to, force):
+    for r in range(3):
+        total = functools.reduce(lambda a, b: a + b, [back[peer, r] for peer in range(back.shape[0])])
+        for k, value in ((2 * r, total), (2 * r + 1, pltpu.roll(total, 64, 1))):
+            target = moved_to if k < 3 else force
+            target[k % 3 : k % 3 + 1] = value[:, 0:64]
 
 
 IN_VMEM = pl.BlockSpec(memory_space=pltpu.VMEM)
@@ -656,8 +664,8 @@
         compiler_params=pltpu.CompilerParams(vmem_limit_bytes=8 * 2**20),
         name="fill_kernel",
     )(part, near(up), near(down))
-    result = jnp.sum(back, 0).reshape(6, 64)
-    return (out, result[:3], result[3:])
+    moved_to, force = run(tail_kernel, (near(back),), (jax.ShapeDtypeStruct((3, 64), F32),) * 2)
+    return (out, moved_to, force)
 
 
 def solution(mesh):

time: 54.5 us -> 54.5 us (level)
  Pallas kernels: 12.8 us -> 13.5 us
  local copies, waits for them, and re-layouts: 0.67 us -> 0 us
    pallas_call x8 -> x9, Pallas kernels: 10.5 us -> 11.2 us  [run(): pl.pallas_call(kernel, out_shape=outs, in_specs=[IN_VMEM] * len(args), ou...]
    slice x1 -> x0, local copies, waits for them, and re-layouts: 0.59 us -> none  [parts(): return (out, result[:3], result[3:])]
where the time goes in v5:
time: 54.5 us; the launch traced here: 54.2 us
  starting transfers between devices  28.5 us (52%)
  Pallas kernels  13.5 us (25%)
  waiting for transfers between devices  11.5 us (21%)
  between operations  0.71 us (1%)
    all_to_all x1, starting transfers between devices, parts(): markers = lax.all_to_all(sent, 'sub', 0, 0, tiled=True)  12.2 us
    pallas_call x9, Pallas kernels, run(): pl.pallas_call(kernel, out_shape=outs, in_specs=[IN_VMEM] * len(args), ou...  11.2 us
    all_to_all x1, waiting for transfers between devices, parts(): markers = lax.all_to_all(sent, 'sub', 0, 0, tiled=True)  9.6 us
    ppermute x2, starting transfers between devices, parts(): down = lax.ppermute(down, 'plate', plate_down)  5.68 us
    all_to_all x1, starting transfers between devices, parts(): back = lax.all_to_all(back, 'sub', 0, 0, tiled=True)  5.67 us
    ppermute x1, starting transfers between devices, parts(): low = lax.ppermute(bottom, 'sub', sub_up)  3.09 us
    all_to_all x1, waiting for transfers between devices, parts(): back = lax.all_to_all(back, 'sub', 0, 0, tiled=True)  1.88 us
    ppermute x2, starting transfers between devices, parts(): up = lax.ppermute(up, 'plate', plate_up)  1.57 us
  transfers between devices with their start and end apart: 8, of which 2 were waited for; matrix products, arithmetic and copies ran while one was open for 0% of the time, Pallas kernels for 14%

profile of v5, /device:TPU:1, one launch (start us, length us, event | category | flops | bytes accessed | tf_op | source)
XLA Modules:
  0.0 54.2 jit_solution(14600943475432661869)
XLA Ops:
  0.6 1.6 %pack_kernel.1 = (f32[32,3,2,128]{3,2,1,0:T(2,128)}, f32[20,4,16,128]{3,2,1,0:T(8,128)S(1)}, f32[456,128]{1,0:T(8,128)S(1)}, f32[456,128]{1,0:T(8,128)S(1)}) custom-call(f32[19,4,16,128]{3,2,1,0:T(8,128)} %own.1, s32[4,16,128]{2,1,0:T(8,128)} %solid.1, s32[3,64]{1,0:T(4,128)} %corner.1, f32[3,64]{1,0:T(4,128)} %frac.1, f32[3,64]{1,0:T(4,128)} %target.1, ...), custom_call_target="tpu_custom_call" | custom-call | tf_op jit(solution)/shard_map/pack_kernel/pallas_call | solution.py:559
  2.2 3.1 %collective-permute-start = (f32[456,128]{1,0:T(8,128)S(1)}, f32[456,128]{1,0:T(8,128)S(1)}, u32[]{:S(2)}, u32[]{:S(2)}) collective-permute-start(f32[456,128]{1,0:T(8,128)S(1)} %get-tuple-element.36), channel_id=1, source_target_pairs={{0,1},{1,2},{2,3},{3,4},{4,5},{5,6},{6,7},{7,8},{8,9},{9,10},{10,1... | collective-permute-start | bytes 700424 | tf_op jit(solution)/shard_map/ppermute | solution.py:580
  5.3 0.3 collective-permute-start.1
  5.6 12.2 %all-to-all-start = ((f32[32,3,2,128]{3,2,1,0:T(2,128)}), f32[32,3,2,128]{3,2,1,0:T(2,128)S(1)}, u32[]{:S(2)}, u32[]{:S(2)}) async-start(f32[32,3,2,128]{3,2,1,0:T(2,128)} %get-tuple-element.44), calls=%async_computation | async-start | bytes 196608 | tf_op jit(solution)/shard_map/all_to_all | solution.py:579
  17.8 0.3 shard_map.94
  18.1 9.6 %all-to-all-done.markers = f32[32,3,2,128]{3,2,1,0:T(2,128)S(1)} async-done(((f32[32,3,2,128]{3,2,1,0:T(2,128)}), f32[32,3,2,128]{3,2,1,0:T(2,128)S(1)}, u32[]{:S(2)}, u32[]{:S(2)}) %all-to-all-start) | async-done | bytes 98336 | tf_op jit(solution)/shard_map/all_to_all | solution.py:579
  27.7 0.9 %shard_map.96 = (bf16[256,2048]{1,0:T(8,128)(2,1)S(1)}, f32[32,2048]{1,0:T(8,128)S(1)}, f32[12,16,128]{2,1,0:T(8,128)S(1)}) custom-call(f32[32,3,2,128]{3,2,1,0:T(2,128)S(1)} %all-to-all-done.markers), custom_call_target="tpu_custom_call" | custom-call | bytes 4000000 | tf_op jit(solution)/shard_map/pallas_call | solution.py:536
  28.6 0.0 collective-permute-done.low
  28.6 0.0 collective-permute-done.1.high
  28.6 0.3 shard_map.95
  28.9 1.9 %shard_map.97 = (f32[5,24,128]{2,1,0:T(8,128)S(1)}, f32[5,24,128]{2,1,0:T(8,128)S(1)}, f32[3,2,32,128]{3,2,1,0:T(8,128)S(1)}, f32[15,16,128]{2,1,0:T(8,128)S(1)}) custom-call(bf16[192,256]{1,0:T(8,128)(2,1)S(1)} %get-tuple-element.42.vown, bf16[192,256]{1,0:T(8,128)(2,1)S(1)} %get-tuple-element.43.vouter, f32[19,4,16,128]{3,2,1,0:T(8,128)S(1)} %get-tuple-element.35.own, ...), custom_call_target="tpu_custom_call" | custom-call | bytes 4000000 | tf_op jit(solution)/shard_map/pallas_call | solution.py:536
  30.8 0.4 collective-permute-start.2
  31.2 3.3 %collective-permute-start.3 = (f32[5,24,128]{2,1,0:T(8,128)S(1)}, f32[5,24,128]{2,1,0:T(8,128)S(1)}, u32[]{:S(2)}, u32[]{:S(2)}) collective-permute-start(f32[5,24,128]{2,1,0:T(8,128)S(1)} %get-tuple-element.53), channel_id=1, source_target_pairs={{32,0},{64,32},{96,64},{128,96},{160,128},{192,160},{224,192},{0,2... | collective-permute-start | bytes 184328 | tf_op jit(solution)/shard_map/ppermute | solution.py:613
  34.4 2.6 %shard_map.98 = (f32[19,2,24,128]{3,2,1,0:T(8,128)S(1)}, f32[3,16,128]{2,1,0:T(8,128)S(1)}, f32[19,2,24,128]{3,2,1,0:T(8,128)}, f32[24,2048]{1,0:T(8,128)S(1)}) custom-call(f32[19,4,16,128]{3,2,1,0:T(8,128)S(1)} %get-tuple-element.35.own, f32[19,4,16,128]{3,2,1,0:T(8,128)S(1)} %get-tuple-element.39.outer, f32[4,32,128]{2,1,0:T(8,128)S(1)} %get-tuple-element.40.fluid, ...), custom_call_target="tpu_custom_call" | custom-call | bytes 12000000 | tf_op jit(solution)/shard_map/pallas_call | solution.py:536
  37.0 0.0 collective-permute-done.2.up
  37.0 0.0 collective-permute-done.3.down
  37.0 1.2 %shard_map.99 = (f32[3,16,128]{2,1,0:T(8,128)S(1)}, f32[2,24,128]{2,1,0:T(8,128)S(1)}, f32[144,128]{1,0:T(8,128)S(1)}, f32[32,3,1,128]{3,2,1,0:T(1,128)}) custom-call(f32[19,2,24,128]{3,2,1,0:T(8,128)S(1)} %get-tuple-element.51.edge, f32[5,24,128]{2,1,0:T(8,128)S(1)} %collective-permute-done.2.up, f32[5,24,128]{2,1,0:T(8,128)S(1)} %collective-permute-done.3.down, ...), custom_call_target="tpu_custom_call" | custom-call | bytes 4000000 | tf_op jit(solution)/shard_map/pallas_call | solution.py:536
  38.2 5.7 %all-to-all-start.1 = ((f32[32,3,1,128]{3,2,1,0:T(1,128)}), f32[32,3,1,128]{3,2,1,0:T(1,128)S(1)}, u32[]{:S(2)}, u32[]{:S(2)}) async-start(f32[32,3,1,128]{3,2,1,0:T(1,128)} %get-tuple-element.62), calls=%async_computation.1 | async-start | bytes 98304 | tf_op jit(solution)/shard_map/all_to_all | solution.py:641
  43.9 0.8 %shard_map.100 = (f32[5,16,128]{2,1,0:T(8,128)S(1)}, f32[5,16,128]{2,1,0:T(8,128)S(1)}, f32[19,2,24,128]{3,2,1,0:T(8,128)S(1)}) custom-call(f32[19,2,24,128]{3,2,1,0:T(8,128)S(1)} %get-tuple-element.51.edge, f32[5,24,128]{2,1,0:T(8,128)S(1)} %collective-permute-done.2.up, f32[5,24,128]{2,1,0:T(8,128)S(1)} %collective-permute-done.3.down, ...), custom_call_target="tpu_custom_call" | custom-call | bytes 4000000 | tf_op jit(solution)/shard_map/pallas_call | solution.py:536
  44.7 1.2 %collective-permute-start.4 = (f32[5,16,128]{2,1,0:T(8,128)S(1)}, f32[5,16,128]{2,1,0:T(8,128)S(1)}, u32[]{:S(2)}, u32[]{:S(2)}) collective-permute-start(f32[5,16,128]{2,1,0:T(8,128)S(1)} %get-tuple-element.60), channel_id=1, source_target_pairs={{0,32},{32,64},{64,96},{96,128},{128,160},{160,192},{192,224},{224... | collective-permute-start | bytes 122888 | tf_op jit(solution)/shard_map/ppermute | solution.py:648
  45.9 2.4 %collective-permute-start.5 = (f32[5,16,128]{2,1,0:T(8,128)S(1)}, f32[5,16,128]{2,1,0:T(8,128)S(1)}, u32[]{:S(2)}, u32[]{:S(2)}) collective-permute-start(f32[5,16,128]{2,1,0:T(8,128)S(1)} %get-tuple-element.61), channel_id=1, source_target_pairs={{32,0},{64,32},{96,64},{128,96},{160,128},{192,160},{224,192},{0,2... | collective-permute-start | bytes 122888 | tf_op jit(solution)/shard_map/ppermute | solution.py:649
  48.3 2.6 %shard_map.101.part = f32[19,4,16,128]{3,2,1,0:T(8,128)} custom-call(f32[19,2,24,128]{3,2,1,0:T(8,128)} %get-tuple-element.50.inside, f32[19,2,24,128]{3,2,1,0:T(8,128)S(1)} %get-tuple-element.59.outside, f32[4,24,128]{2,1,0:T(8,128)S(1)} %get-tuple-element.41.fluid_inner.fluid, f32[3,16,128]{2,1,0:T(8,128)S(1)} %get-tuple-element.58.force, ...), custom_call_target="tpu_custom_call" | custom-call | bytes 12000000 | tf_op jit(solution)/shard_map/pallas_call | solution.py:536
  50.9 0.0 collective-permute-done.4.up
  50.9 0.0 collective-permute-done.5.down
  50.9 0.7 %fill_kernel.1 = f32[19,4,16,128]{3,2,1,0:T(8,128)} custom-call(f32[19,4,16,128]{3,2,1,0:T(8,128)} %shard_map.101.part, f32[5,16,128]{2,1,0:T(8,128)S(1)} %collective-permute-done.4.up, f32[5,16,128]{2,1,0:T(8,128)S(1)} %collective-permute-done.5.down), custom_call_target="tpu_custom_call", output_to_operand_aliasing={{}: (0, {})} | custom-call | tf_op jit(solution)/shard_map/fill_kernel/pallas_call | solution.py:657
  51.6 1.9 %all-to-all-done.1.back = f32[32,3,1,128]{3,2,1,0:T(1,128)S(1)} async-done(((f32[32,3,1,128]{3,2,1,0:T(1,128)}), f32[32,3,1,128]{3,2,1,0:T(1,128)S(1)}, u32[]{:S(2)}, u32[]{:S(2)}) %all-to-all-start.1) | async-done | bytes 49184 | tf_op jit(solution)/shard_map/all_to_all | solution.py:641
  53.5 0.7 %shard_map.102 = (f32[3,64]{1,0:T(4,128)}, f32[3,64]{1,0:T(4,128)}) custom-call(f32[32,3,1,128]{3,2,1,0:T(1,128)S(1)} %all-to-all-done.1.back), custom_call_target="tpu_custom_call" | custom-call | bytes 4000000 | tf_op jit(solution)/shard_map/pallas_call | solution.py:536
Async XLA Ops:
  2.2 26.4 %collective-permute-start = (f32[456,128]{1,0:T(8,128)S(1)}, f32[456,128]{1,0:T(8,128)S(1)}, u32[]{:S(2)}, u32[]{:S(2)}) collective-permute-start(f32[456,128]{1,0:T(8,128)S(1)} %get-tuple-element.36), channel_id=1, source_target_pairs={{0,1},{1,2},{2,3},{3,4},{4,5},{5,6},{6,7},{7,8},{8,9},{9,10},{10,1... | collective-permute-start | bytes 700424 | tf_op jit(solution)/shard_map/ppermute | solution.py:580
  5.3 23.3 %collective-permute-start.1 = (f32[456,128]{1,0:T(8,128)S(1)}, f32[456,128]{1,0:T(8,128)S(1)}, u32[]{:S(2)}, u32[]{:S(2)}) collective-permute-start(f32[456,128]{1,0:T(8,128)S(1)} %get-tuple-element.38), channel_id=1, source_target_pairs={{1,0},{2,1},{3,2},{4,3},{5,4},{6,5},{7,6},{8,7},{9,8},{10,9},{11,1... | collective-permute-start | bytes 700424 | tf_op jit(solution)/shard_map/ppermute | solution.py:581
  5.6 22.1 %all-to-all-start = ((f32[32,3,2,128]{3,2,1,0:T(2,128)}), f32[32,3,2,128]{3,2,1,0:T(2,128)S(1)}, u32[]{:S(2)}, u32[]{:S(2)}) async-start(f32[32,3,2,128]{3,2,1,0:T(2,128)} %get-tuple-element.44), calls=%async_computation | async-start | bytes 196608 | tf_op jit(solution)/shard_map/all_to_all | solution.py:579
  30.8 6.2 %collective-permute-start.2 = (f32[5,24,128]{2,1,0:T(8,128)S(1)}, f32[5,24,128]{2,1,0:T(8,128)S(1)}, u32[]{:S(2)}, u32[]{:S(2)}) collective-permute-start(f32[5,24,128]{2,1,0:T(8,128)S(1)} %get-tuple-element.52), channel_id=1, source_target_pairs={{0,32},{32,64},{64,96},{96,128},{128,160},{160,192},{192,224},{224... | collective-permute-start | bytes 184328 | tf_op jit(solution)/shard_map/ppermute | solution.py:612
  31.2 5.9 %collective-permute-start.3 = (f32[5,24,128]{2,1,0:T(8,128)S(1)}, f32[5,24,128]{2,1,0:T(8,128)S(1)}, u32[]{:S(2)}, u32[]{:S(2)}) collective-permute-start(f32[5,24,128]{2,1,0:T(8,128)S(1)} %get-tuple-element.53), channel_id=1, source_target_pairs={{32,0},{64,32},{96,64},{128,96},{160,128},{192,160},{224,192},{0,2... | collective-permute-start | bytes 184328 | tf_op jit(solution)/shard_map/ppermute | solution.py:613
  38.2 15.3 %all-to-all-start.1 = ((f32[32,3,1,128]{3,2,1,0:T(1,128)}), f32[32,3,1,128]{3,2,1,0:T(1,128)S(1)}, u32[]{:S(2)}, u32[]{:S(2)}) async-start(f32[32,3,1,128]{3,2,1,0:T(1,128)} %get-tuple-element.62), calls=%async_computation.1 | async-start | bytes 98304 | tf_op jit(solution)/shard_map/all_to_all | solution.py:641
  44.7 6.2 %collective-permute-start.4 = (f32[5,16,128]{2,1,0:T(8,128)S(1)}, f32[5,16,128]{2,1,0:T(8,128)S(1)}, u32[]{:S(2)}, u32[]{:S(2)}) collective-permute-start(f32[5,16,128]{2,1,0:T(8,128)S(1)} %get-tuple-element.60), channel_id=1, source_target_pairs={{0,32},{32,64},{64,96},{96,128},{128,160},{160,192},{192,224},{224... | collective-permute-start | bytes 122888 | tf_op jit(solution)/shard_map/ppermute | solution.py:648
  45.9 5.0 %collective-permute-start.5 = (f32[5,16,128]{2,1,0:T(8,128)S(1)}, f32[5,16,128]{2,1,0:T(8,128)S(1)}, u32[]{:S(2)}, u32[]{:S(2)}) collective-permute-start(f32[5,16,128]{2,1,0:T(8,128)S(1)} %get-tuple-element.61), channel_id=1, source_target_pairs={{32,0},{64,32},{96,64},{128,96},{160,128},{192,160},{224,192},{0,2... | collective-permute-start | bytes 122888 | tf_op jit(solution)/shard_map/ppermute | solution.py:649
